TPU v7x, 32 devices: a whole 2x2x4 slice. The times are simulated.
32 devices in a mesh: parts: 2 (over y), shard: 4 (over z), layer: 2 (over x), sub: 2 (over core).
Axes of the slice: x: 2, y: 2, z: 4, core: 2. Of those that a mesh axis runs over, the one named last changes fastest.
Arguments:
- act_in: bfloat16 [2, 1024, 14336], P('layer', ('parts', 'shard'), 'sub'), parts along dimension 1, may hold values from -6 to 6
- grad_out: bfloat16 [2, 1024, 8192], P('layer', ('parts', 'shard'), 'sub'), parts along dimension 1, may hold values from -6 to 6
- factor_in: bfloat16 [2, 12, 32, 14336], P('layer', 'shard', None, 'sub'), may hold values from -0.046875 to 0.046875
- factor_out: bfloat16 [2, 12, 32, 8192], P('layer', 'shard', None, 'sub'), may hold values from -0.0625 to 0.0625
- query_row: int32 [12], replicated, may hold values from 0 to 11, as said below
- pairs: int32 [2, 4, 12], replicated, may hold values from 0 to 1, as said below
Outputs:
- scores: float32 [1024, 12], P(('parts', 'shard'), 'layer'), parts along dimension 0
There are 2 independent parts, one for each index of `parts`. A program takes and returns all parts, laid end to end along the dimension named above; an argument that names none is the same for every part. Nothing has to cross between parts.
Inputs may be any that keep to these rules, and one draw needn't show every extreme that they name: A permutation: query q's factors are row query_row[q] of factor_in and factor_out. `pairs`: for each layer, shard and k, at most one listed query has its stored row in k * 3 to (k + 1) * 3 - 1; in every layer some shard lists one query for every k.
All inputs are finite; a program needn't handle non-finite values.
Results may differ from a plain program's by a relative error of at most 0.0003.
Values may be sent and summed in bfloat16 or wider, within the bound.
No kernel may reach another device: no remote copies, remote signals or barrier semaphores. Data moves between devices by JAX's collectives and lax.ppermute only.
A program may use at most 64 MiB of HBM per device.

v0:
```python
import functools
import itertools

import jax
import jax.numpy as jnp
from jax import lax
from jax.experimental import pallas as pl
from jax.experimental.pallas import tpu as pltpu
from jax.sharding import PartitionSpec as P


def shifted(sizes, shift):
    places = list(itertools.product(*[range(n) for n in sizes]))
    return [
        (i, places.index(tuple((a + b) % n for a, b, n in zip(place, shift, sizes)))) for i, place in enumerate(places)
    ]


def wrap(i, n):
    return jnp.where(i >= n, i - n, i)


def dest(shard, j, n):
    if n & (n - 1) == 0:
        return shard ^ j
    return (shard + j) % n


def source(shard, j, n):
    if n & (n - 1) == 0:
        return shard ^ j
    return (shard + n - j) % n


def slot_groups(n):
    late = list(range(max(1, n // 2), n))
    return [j for j in range(n) if j not in late], late


def start_tables(query_hbm, pairs_hbm, query_row, pairs, sem):
    copies = [pltpu.make_async_copy(query_hbm, query_row, sem.at[0]), pltpu.make_async_copy(pairs_hbm, pairs, sem.at[1])]
    for copy in copies:
        copy.start()
    return copies


def table_scratch(query_row, pairs):
    return [pltpu.SMEM(query_row.shape, query_row.dtype), pltpu.SMEM(pairs.shape, pairs.dtype)]


def pick_rows(query_row, pairs, per_owner, dests):
    base = lax.axis_index("shard") * per_owner
    layer = lax.axis_index("layer")

    def step(q, rows):
        row = query_row[q] - base
        held = jnp.logical_and(row >= 0, row < per_owner)
        row = jnp.where(held, row, 0)
        return tuple(r + pairs[layer, to, q] * row for r, to in zip(rows, dests))

    count = query_row.shape[0]
    rows = lax.fori_loop(0, count, step, (jnp.int32(0),) * len(dests), unroll=count <= 16)
    return [jnp.clip(row, 0, per_owner - 1) for row in rows]


def span(part, wide):
    return pl.ds(pl.multiple_of(part * wide, 128), wide)


def send_kernel(parts, shard_count, query_hbm, pairs_hbm, act, grad, factor_in, factor_out, *refs):
    sent, (query_row, pairs, stored, sem, table_sem) = refs[:-5], refs[-5:]
    tables = start_tables(query_hbm, pairs_hbm, query_row, pairs, table_sem)
    my_part, my_shard = lax.axis_index("parts"), lax.axis_index("shard")
    wide_out, wide_in = grad.shape[2] // parts, act.shape[2] // parts
    to_out, to_in = pl.ds(0, wide_out), pl.ds(wide_out, wide_in)
    copies = []

    def start(piece, target):
        copies.append(pltpu.make_async_copy(piece, target, sem.at[len(copies)]))
        copies[-1].start()

    start(factor_out.at[0, :, :, span(my_part, wide_out)], stored.at[:, :, to_out])
    start(factor_in.at[0, :, :, span(my_part, wide_in)], stored.at[:, :, to_in])
    for e in range(1, parts):
        part = wrap(my_part + e, parts)
        start(grad.at[0, :, span(part, wide_out)], sent[shard_count - 1 + e - 1].at[:, to_out])
        start(act.at[0, :, span(part, wide_in)], sent[shard_count - 1 + e - 1].at[:, to_in])
    for table in tables:
        table.wait()
    dests = [dest(my_shard, j, shard_count) for j in range(1, shard_count)]
    listed = pick_rows(query_row, pairs, factor_out.shape[1], dests)
    for copy in copies[:2]:
        copy.wait()
    for target, row in zip(sent, listed):
        target[...] = stored[row]
    for copy in copies[2:]:
        copy.wait()


def make_sends(act, grad, factor_in, factor_out, query_row, pairs):
    parts, shard_count = lax.axis_size("parts"), lax.axis_size("shard")
    rank, tokens = factor_out.shape[2], act.shape[1]
    wide = (grad.shape[2] + act.shape[2]) // parts
    shapes = [pltpu.VMEM((rank, wide), act.dtype)] * (shard_count - 1)
    shapes += [pltpu.VMEM((tokens, wide), act.dtype)] * (parts - 1)
    sent = pl.pallas_call(
        functools.partial(send_kernel, parts, shard_count),
        out_shape=shapes,
        in_specs=[pl.BlockSpec(memory_space=pltpu.HBM)] * 6,
        out_specs=[pl.BlockSpec(memory_space=pltpu.VMEM)] * len(shapes),
        scratch_shapes=table_scratch(query_row, pairs)
        + [
            pltpu.VMEM((factor_out.shape[1], rank, wide), act.dtype),
            pltpu.SemaphoreType.DMA((2 * parts,)),
            pltpu.SemaphoreType.DMA((2,)),
        ],
        compiler_params=pltpu.CompilerParams(vmem_limit_bytes=2**23),
        name="make_sends",
    )(query_row, pairs, act, grad, factor_in, factor_out)
    return sent[: shard_count - 1], sent[shard_count - 1 :]


def own_kernel(parts, order, query_hbm, pairs_hbm, act, grad, factor_in, factor_out, rows, slot, weights, *scratch):
    query_row, pairs, sem, table_sem = scratch
    tables = start_tables(query_hbm, pairs_hbm, query_row, pairs, table_sem)
    my_part, my_shard, my_layer = lax.axis_index("parts"), lax.axis_index("shard"), lax.axis_index("layer")
    layers, shard_count = lax.axis_size("layer"), lax.axis_size("shard")
    per_owner, tokens = factor_out.shape[1], rows.shape[0]
    wide_out, wide_in = grad.shape[2] // parts, act.shape[2] // parts
    span_out, span_in = span(my_part, wide_out), span(my_part, wide_in)
    to_out, to_in = pl.ds(0, wide_out), pl.ds(wide_out, wide_in)
    copies = [
        pltpu.make_async_copy(grad.at[0, :, span_out], rows.at[:, to_out], sem.at[0]),
        pltpu.make_async_copy(act.at[0, :, span_in], rows.at[:, to_in], sem.at[1]),
    ]
    for copy in copies:
        copy.start()
    for table in tables:
        table.wait()
    (row,) = pick_rows(query_row, pairs, per_owner, [my_shard])
    copies += [
        pltpu.make_async_copy(factor_out.at[0, row, :, span_out], slot.at[:, to_out], sem.at[2]),
        pltpu.make_async_copy(factor_in.at[0, row, :, span_in], slot.at[:, to_in], sem.at[3]),
    ]
    for copy in copies[2:]:
        copy.start()
    wide = query_row.shape[0] // layers
    for e in range(layers):
        layer = wrap(my_layer + e, layers)
        for i in range(wide):
            q = layer * wide + i
            listed = pairs[my_layer, my_shard, q]
            for k, j in enumerate(order):
                row = query_row[q] - source(my_shard, j, shard_count) * per_owner
                here = jnp.logical_and(row >= 0, row < per_owner)
                weight = jnp.where(here, listed, 0).astype(jnp.float32)
                weights[e, k, i : i + 1, :] = jnp.full((1, tokens), weight, jnp.float32)
    for copy in copies:
        copy.wait()


def make_own(order, act, grad, factor_in, factor_out, query_row, pairs):
    parts, layers = lax.axis_size("parts"), lax.axis_size("layer")
    rank, tokens = factor_out.shape[2], act.shape[1]
    wide = (grad.shape[2] + act.shape[2]) // parts
    shapes = [
        pltpu.VMEM((tokens, wide), act.dtype),
        pltpu.VMEM((rank, wide), act.dtype),
        pltpu.VMEM((layers, len(order), query_row.shape[0] // layers, tokens), jnp.float32),
    ]
    return pl.pallas_call(
        functools.partial(own_kernel, parts, tuple(order)),
        out_shape=shapes,
        in_specs=[pl.BlockSpec(memory_space=pltpu.HBM)] * 6,
        out_specs=[pl.BlockSpec(memory_space=pltpu.VMEM)] * len(shapes),
        scratch_shapes=table_scratch(query_row, pairs) + [pltpu.SemaphoreType.DMA((4,)), pltpu.SemaphoreType.DMA((2,))],
        compiler_params=pltpu.CompilerParams(vmem_limit_bytes=2**22),
        name="make_own",
    )(query_row, pairs, act, grad, factor_in, factor_out)


def project_kernel(slot_count, wide_out, *refs):
    slots, rest = refs[:slot_count], refs[slot_count:]
    blocks, outs = rest[: len(rest) // 2], rest[len(rest) // 2 :]
    dims = (((1,), (1,)), ((), ()))
    rank, wide = slots[0].shape
    for which, (low, high) in enumerate(((0, wide_out), (wide_out, wide))):
        left = jnp.concatenate([slot[:, low:high] for slot in slots], axis=0)
        for block, out in zip(blocks, outs):
            proj = lax.dot_general(left, block[:, low:high], dims, preferred_element_type=jnp.float32)
            for j in range(slot_count):
                out[which, j] = proj[j * rank : (j + 1) * rank]


def project(slots, blocks, wide_out):
    vmem = pl.BlockSpec(memory_space=pltpu.VMEM)
    (rank, wide), tokens = slots[0].shape, blocks[0].shape[0]
    inputs = [pltpu.with_memory_space_constraint(x, pltpu.VMEM) for x in (*slots, *blocks)]
    flops = 2 * len(slots) * rank * len(blocks) * tokens * wide
    read = 2 * wide * (len(slots) * rank + len(blocks) * tokens)
    return pl.pallas_call(
        functools.partial(project_kernel, len(slots), wide_out),
        out_shape=[pltpu.VMEM((2, len(slots), rank, tokens), jnp.float32)] * len(blocks),
        in_specs=[vmem] * len(inputs),
        out_specs=[vmem] * len(blocks),
        compiler_params=pltpu.CompilerParams(vmem_limit_bytes=2**23),
        cost_estimate=pl.CostEstimate(flops=flops, bytes_accessed=read, transcendentals=0),
        name="project",
    )(*inputs)


def join_kernel(*refs):
    early, late, out = refs[:-2], refs[-2], refs[-1]
    total = early[0][...]
    for piece in early[1:]:
        total = total + piece[...]
    out[:, : total.shape[1]] = total
    out[:, total.shape[1] :] = late[...]


def join(early, late):
    vmem = pl.BlockSpec(memory_space=pltpu.VMEM)
    inputs = [pltpu.with_memory_space_constraint(x, pltpu.VMEM) for x in (*early, late)]
    return pl.pallas_call(
        join_kernel,
        out_shape=pltpu.VMEM((2, early[0].shape[1] + late.shape[1], *late.shape[2:]), jnp.float32),
        in_specs=[vmem] * len(inputs),
        out_specs=vmem,
        compiler_params=pltpu.CompilerParams(vmem_limit_bytes=2**23),
        name="join",
    )(*inputs)


def score_kernel(done, whole_count, weights, *refs):
    layers = weights.shape[0]
    pieces, outs = refs[:-layers], refs[-layers:]
    whole, parted = pieces[:whole_count], pieces[whole_count:]
    total = whole[0][...]
    for piece in whole[1:]:
        total = total + piece[...]
    first, last = total[:, :done], total[:, done:]
    if parted:
        more = parted[0][...]
        for piece in parted[1:]:
            more = more + piece[...]
        last = last + more
    scores = [jnp.sum(t[0, k] * t[1, k], axis=0, keepdims=True) for t in (first, last) for k in range(t.shape[1])]
    for e, out in enumerate(outs):
        block = weights[e, 0] * scores[0]
        for k in range(1, len(scores)):
            block = block + weights[e, k] * scores[k]
        out[...] = block


def make_scores(weights, whole, parted):
    layers, count, wide, tokens = weights.shape
    vmem = pl.BlockSpec(memory_space=pltpu.VMEM)
    inputs = [pltpu.with_memory_space_constraint(x, pltpu.VMEM) for x in (weights, *whole, *parted)]
    done = count - (parted[0].shape[1] if parted else 0)
    return pl.pallas_call(
        functools.partial(score_kernel, done, len(whole)),
        out_shape=[pltpu.VMEM((wide, tokens), jnp.float32)] * layers,
        in_specs=[vmem] * len(inputs),
        out_specs=[vmem] * layers,
        compiler_params=pltpu.CompilerParams(vmem_limit_bytes=2**23),
        name="make_scores",
    )(*inputs)


def shards(act_in, grad_out, factor_in, factor_out, query_row, pairs):
    parts = lax.axis_size("parts")
    shard_count = lax.axis_size("shard")
    layers = lax.axis_size("layer")
    subs = lax.axis_size("sub")
    wide_out = grad_out.shape[2] // parts
    early, late = slot_groups(shard_count)

    args = [
        pltpu.with_memory_space_constraint(x, pltpu.HBM)
        for x in (act_in, grad_out, factor_in, factor_out, query_row, pairs)
    ]
    sent_slots, sent_rows = make_sends(*args)
    rows = []
    for e in range(1, parts):
        rows.append(lax.ppermute(sent_rows[e - 1], "parts", shifted((parts,), (e,))))
    slots = [None] * shard_count
    for j in late[::-1] + early[1:]:
        to = [(i, dest(i, j, shard_count)) for i in range(shard_count)]
        slots[j] = lax.ppermute(sent_slots[j - 1], "shard", to)
    own_rows, slots[0], weights = make_own(early + late, *args)

    early_own = project([slots[j] for j in early], [own_rows], wide_out)
    early_rest = project([slots[j] for j in early], rows, wide_out) if rows else []
    early_got, late_got = [], []
    for e, block in enumerate(early_rest, 1):
        early_got.append(lax.ppermute(block, "parts", shifted((parts,), (parts - e,))))
    late_rest = project([slots[j] for j in late], rows, wide_out) if rows else []
    for e, block in enumerate(late_rest, 1):
        for f in range(subs):
            late_got.append(lax.ppermute(block, ("parts", "sub"), shifted((parts, subs), (parts - e, f))))
    (late_own,) = project([slots[j] for j in late], [own_rows], wide_out)
    whole = [join(list(early_own) + early_got, late_own)]
    for f in range(1, subs):
        whole.append(lax.ppermute(whole[0], "sub", shifted((subs,), (f,))))
    blocks = make_scores(weights, whole, late_got)

    out = blocks[0]
    for e in range(1, layers):
        out = out + lax.ppermute(blocks[e], "layer", shifted((layers,), (e,)))
    return out.T


def solution(mesh):
    in_specs = (
        P("layer", ("parts", "shard"), "sub"),
        P("layer", ("parts", "shard"), "sub"),
        P("layer", "shard", None, "sub"),
        P("layer", "shard", None, "sub"),
        P(),
        P(),
    )
    out_specs = P(("parts", "shard"), "layer")

    return jax.shard_map(shards, mesh=mesh, in_specs=in_specs, out_specs=out_specs, check_vma=False)
```

profile of v0, /device:TPU:0, one launch (start us, length us, event | category | flops | bytes accessed | tf_op | source)
XLA Modules:
  0.0 52.5 jit_solution(14168161472575296690)
XLA Ops:
  0.0 1.7 %make_sends.1 = (bf16[32,5632]{1,0:T(8,128)(2,1)S(1)}, bf16[32,5632]{1,0:T(8,128)(2,1)S(1)}, bf16[32,5632]{1,0:T(8,128)(2,1)S(1)}, bf16[128,5632]{1,0:T(8,128)(2,1)S(1)}) custom-call(s32[12]{0:T(128)} %query_hbm.3, s32[2,4,12]{2,1,0:T(4,128)} %pairs_hbm.3, bf16[1,128,7168]{2,1,0:T(8,128)(2,1)} %act.3, bf16[1,128,4096]{2,1,0:T(8,128)(2,1)} %grad.3, ...), custom_call_target="tpu_custom_call" | custom-call | tf_op jit(solution)/shard_map/make_sends/pallas_call | solution.py:106
  1.7 3.1 %collective-permute-start.1 = (bf16[128,5632]{1,0:T(8,128)(2,1)S(1)}, bf16[128,5632]{1,0:T(8,128)(2,1)S(1)}, u32[]{:S(2)}, u32[]{:S(2)}) collective-permute-start(bf16[128,5632]{1,0:T(8,128)(2,1)S(1)} %get-tuple-element.18), channel_id=1, source_target_pairs={{0,16},{16,0},{1,17},{17,1},{2,18},{18,2},{3,19},{19,3},{4,20},{20... | collective-permute-start | bytes 4325384 | tf_op jit(solution)/shard_map/ppermute | solution.py:285
  4.8 1.6 %collective-permute-start = (bf16[32,5632]{1,0:T(8,128)(2,1)S(1)}, bf16[32,5632]{1,0:T(8,128)(2,1)S(1)}, u32[]{:S(2)}, u32[]{:S(2)}) collective-permute-start(bf16[32,5632]{1,0:T(8,128)(2,1)S(1)} %get-tuple-element.16), channel_id=1, source_target_pairs={{0,4},{4,0},{8,12},{12,8},{1,5},{5,1},{9,13},{13,9},{2,6},{6,2},{1... | collective-permute-start | bytes 1081352 | tf_op jit(solution)/shard_map/ppermute | solution.py:289
  6.4 2.6 %collective-permute-start.3 = (bf16[32,5632]{1,0:T(8,128)(2,1)S(1)}, bf16[32,5632]{1,0:T(8,128)(2,1)S(1)}, u32[]{:S(2)}, u32[]{:S(2)}) collective-permute-start(bf16[32,5632]{1,0:T(8,128)(2,1)S(1)} %get-tuple-element.19), channel_id=1, source_target_pairs={{0,8},{4,12},{8,0},{12,4},{1,9},{5,13},{9,1},{13,5},{2,10},{6,14},... | collective-permute-start | bytes 1081352 | tf_op jit(solution)/shard_map/ppermute | solution.py:289
  9.0 0.2 collective-permute-start.4
  9.2 1.9 %make_own.1 = (bf16[128,5632]{1,0:T(8,128)(2,1)S(1)}, bf16[32,5632]{1,0:T(8,128)(2,1)S(1)}, f32[2,4,6,128]{3,2,1,0:T(8,128)S(1)}) custom-call(s32[12]{0:T(128)} %query_hbm.3, s32[2,4,12]{2,1,0:T(4,128)} %pairs_hbm.3, bf16[1,128,7168]{2,1,0:T(8,128)(2,1)} %act.3, bf16[1,128,4096]{2,1,0:T(8,128)(2,1)} %grad.3, bf16[1,3,32,7168]{3,2,1,0:T(8,128)(2,1)} %factor_in.3, ...), custom_call_target="tpu_custom_call" | custom-call | tf_op jit(solution)/shard_map/make_own/pallas_call | solution.py:171
  11.1 10.4 %collective-permute-done.refs_1_ = bf16[32,5632]{1,0:T(8,128)(2,1)S(1)} collective-permute-done((bf16[32,5632]{1,0:T(8,128)(2,1)S(1)}, bf16[32,5632]{1,0:T(8,128)(2,1)S(1)}, u32[]{:S(2)}, u32[]{:S(2)}) %collective-permute-start) | collective-permute-done | bytes 360480 | tf_op jit(solution)/shard_map/ppermute | solution.py:289
  21.5 14.9 %collective-permute-done.1.refs_2_ = bf16[128,5632]{1,0:T(8,128)(2,1)S(1)} collective-permute-done((bf16[128,5632]{1,0:T(8,128)(2,1)S(1)}, bf16[128,5632]{1,0:T(8,128)(2,1)S(1)}, u32[]{:S(2)}, u32[]{:S(2)}) %collective-permute-start.1) | collective-permute-done | bytes 1441824 | tf_op jit(solution)/shard_map/ppermute | solution.py:285
  36.4 0.6 %project.5 = f32[2,2,32,128]{3,2,1,0:T(8,128)S(1)} custom-call(bf16[32,5632]{1,0:T(8,128)(2,1)S(1)} %get-tuple-element.15.refs_0_, bf16[32,5632]{1,0:T(8,128)(2,1)S(1)} %collective-permute-done.refs_1_, bf16[128,5632]{1,0:T(8,128)(2,1)S(1)} %collective-permute-done.1.refs_2_), custom_call_target="tpu_custom_call" | custom-call | flops 92274688 | bytes 2162688 | tf_op jit(solution)/shard_map/project/pallas_call | solution.py:201
  37.0 1.8 %collective-permute-start.2 = (f32[2,2,32,128]{3,2,1,0:T(8,128)S(1)}, f32[2,2,32,128]{3,2,1,0:T(8,128)S(1)}, u32[]{:S(2)}, u32[]{:S(2)}) collective-permute-start(f32[2,2,32,128]{3,2,1,0:T(8,128)S(1)} %project.5), channel_id=1, source_target_pairs={{0,16},{16,0},{1,17},{17,1},{2,18},{18,2},{3,19},{19,3},{4,20},{20... | collective-permute-start | bytes 196616 | tf_op jit(solution)/shard_map/ppermute | solution.py:296
  38.8 0.6 %project.4.refs_0_ = f32[2,2,32,128]{3,2,1,0:T(8,128)S(1)} custom-call(bf16[32,5632]{1,0:T(8,128)(2,1)S(1)} %get-tuple-element.15.refs_0_, bf16[32,5632]{1,0:T(8,128)(2,1)S(1)} %collective-permute-done.refs_1_, bf16[128,5632]{1,0:T(8,128)(2,1)S(1)} %get-tuple-element.17.refs_2_), custom_call_target="tpu_custom_call" | custom-call | flops 92274688 | bytes 2162688 | tf_op jit(solution)/shard_map/project/pallas_call | solution.py:201
  39.4 0.0 collective-permute-done.3.refs_0_
  39.4 0.0 collective-permute-done.4.refs_1_
  39.4 0.6 %project.6.refs_2_ = f32[2,2,32,128]{3,2,1,0:T(8,128)S(1)} custom-call(bf16[32,5632]{1,0:T(8,128)(2,1)S(1)} %collective-permute-done.3.refs_0_, bf16[32,5632]{1,0:T(8,128)(2,1)S(1)} %collective-permute-done.4.refs_1_, bf16[128,5632]{1,0:T(8,128)(2,1)S(1)} %get-tuple-element.17.refs_2_), custom_call_target="tpu_custom_call" | custom-call | flops 92274688 | bytes 2162688 | tf_op jit(solution)/shard_map/project/pallas_call | solution.py:201
  40.0 1.3 %collective-permute-done.2.refs_1_ = f32[2,2,32,128]{3,2,1,0:T(8,128)S(1)} collective-permute-done((f32[2,2,32,128]{3,2,1,0:T(8,128)S(1)}, f32[2,2,32,128]{3,2,1,0:T(8,128)S(1)}, u32[]{:S(2)}, u32[]{:S(2)}) %collective-permute-start.2) | collective-permute-done | bytes 65568 | tf_op jit(solution)/shard_map/ppermute | solution.py:296
  41.3 0.1 collective-permute-start.5
  41.4 0.6 %project.7 = f32[2,2,32,128]{3,2,1,0:T(8,128)S(1)} custom-call(bf16[32,5632]{1,0:T(8,128)(2,1)S(1)} %collective-permute-done.3.refs_0_, bf16[32,5632]{1,0:T(8,128)(2,1)S(1)} %collective-permute-done.4.refs_1_, bf16[128,5632]{1,0:T(8,128)(2,1)S(1)} %collective-permute-done.1.refs_2_), custom_call_target="tpu_custom_call" | custom-call | flops 92274688 | bytes 2162688 | tf_op jit(solution)/shard_map/project/pallas_call | solution.py:201
  42.0 1.9 %collective-permute-start.7 = (f32[2,2,32,128]{3,2,1,0:T(8,128)S(1)}, f32[2,2,32,128]{3,2,1,0:T(8,128)S(1)}, u32[]{:S(2)}, u32[]{:S(2)}) collective-permute-start(f32[2,2,32,128]{3,2,1,0:T(8,128)S(1)} %project.7), channel_id=1, source_target_pairs={{0,17},{1,16},{16,1},{17,0},{2,19},{3,18},{18,3},{19,2},{4,21},{5,... | collective-permute-start | bytes 196616 | tf_op jit(solution)/shard_map/ppermute | solution.py:300
  43.9 0.3 collective-permute-start.6
  44.2 2.2 %collective-permute-done.7.refs_3_ = f32[2,2,32,128]{3,2,1,0:T(8,128)S(1)} collective-permute-done((f32[2,2,32,128]{3,2,1,0:T(8,128)S(1)}, f32[2,2,32,128]{3,2,1,0:T(8,128)S(1)}, u32[]{:S(2)}, u32[]{:S(2)}) %collective-permute-start.7) | collective-permute-done | bytes 65568 | tf_op jit(solution)/shard_map/ppermute | solution.py:300
  46.4 1.8 %collective-permute-done.6.refs_2_ = f32[2,2,32,128]{3,2,1,0:T(8,128)S(1)} collective-permute-done((f32[2,2,32,128]{3,2,1,0:T(8,128)S(1)}, f32[2,2,32,128]{3,2,1,0:T(8,128)S(1)}, u32[]{:S(2)}, u32[]{:S(2)}) %collective-permute-start.6) | collective-permute-done | bytes 65568 | tf_op jit(solution)/shard_map/ppermute | solution.py:300
  48.2 0.0 collective-permute-done.5.refs_1_
  48.2 1.6 %collective-permute-start.8 = (f32[6,128]{1,0:T(8,128)S(1)}, f32[6,128]{1,0:T(8,128)S(1)}, u32[]{:S(2)}, u32[]{:S(2)}) collective-permute-start(f32[6,128]{1,0:T(8,128)S(1)} %get-tuple-element.22), channel_id=1, source_target_pairs={{0,2},{2,0},{1,3},{3,1},{4,6},{6,4},{5,7},{7,5},{8,10},{10,8},{9,1... | collective-permute-start | bytes 9224 | tf_op jit(solution)/shard_map/ppermute | solution.py:309
  49.8 2.1 %collective-permute-done.8 = f32[6,128]{1,0:T(8,128)S(1)} collective-permute-done((f32[6,128]{1,0:T(8,128)S(1)}, f32[6,128]{1,0:T(8,128)S(1)}, u32[]{:S(2)}, u32[]{:S(2)}) %collective-permute-start.8) | collective-permute-done | bytes 3104 | tf_op jit(solution)/shard_map/ppermute | solution.py:309
  51.9 0.6 %add_bitcast_fusion = f32[128,6]{0,1:T(8,128)} fusion(f32[6,128]{1,0:T(8,128)S(1)} %get-tuple-element.21, f32[6,128]{1,0:T(8,128)S(1)} %collective-permute-done.8), kind=kLoop, calls=%fused_computation | loop fusion | flops 768 | bytes 9216 | tf_op jit(solution)/shard_map/transpose | solution.py:310
  (2 shorter events, 0.1 us)
Async XLA Ops:
  1.7 34.6 %collective-permute-start.1 = (bf16[128,5632]{1,0:T(8,128)(2,1)S(1)}, bf16[128,5632]{1,0:T(8,128)(2,1)S(1)}, u32[]{:S(2)}, u32[]{:S(2)}) collective-permute-start(bf16[128,5632]{1,0:T(8,128)(2,1)S(1)} %get-tuple-element.18), channel_id=1, source_target_pairs={{0,16},{16,0},{1,17},{17,1},{2,18},{18,2},{3,19},{19,3},{4,20},{20... | collective-permute-start | bytes 4325384 | tf_op jit(solution)/shard_map/ppermute | solution.py:285
  4.8 16.7 %collective-permute-start = (bf16[32,5632]{1,0:T(8,128)(2,1)S(1)}, bf16[32,5632]{1,0:T(8,128)(2,1)S(1)}, u32[]{:S(2)}, u32[]{:S(2)}) collective-permute-start(bf16[32,5632]{1,0:T(8,128)(2,1)S(1)} %get-tuple-element.16), channel_id=1, source_target_pairs={{0,4},{4,0},{8,12},{12,8},{1,5},{5,1},{9,13},{13,9},{2,6},{6,2},{1... | collective-permute-start | bytes 1081352 | tf_op jit(solution)/shard_map/ppermute | solution.py:289
  6.4 33.0 %collective-permute-start.3 = (bf16[32,5632]{1,0:T(8,128)(2,1)S(1)}, bf16[32,5632]{1,0:T(8,128)(2,1)S(1)}, u32[]{:S(2)}, u32[]{:S(2)}) collective-permute-start(bf16[32,5632]{1,0:T(8,128)(2,1)S(1)} %get-tuple-element.19), channel_id=1, source_target_pairs={{0,8},{4,12},{8,0},{12,4},{1,9},{5,13},{9,1},{13,5},{2,10},{6,14},... | collective-permute-start | bytes 1081352 | tf_op jit(solution)/shard_map/ppermute | solution.py:289
  9.0 30.4 %collective-permute-start.4 = (bf16[32,5632]{1,0:T(8,128)(2,1)S(1)}, bf16[32,5632]{1,0:T(8,128)(2,1)S(1)}, u32[]{:S(2)}, u32[]{:S(2)}) collective-permute-start(bf16[32,5632]{1,0:T(8,128)(2,1)S(1)} %get-tuple-element.20), channel_id=1, source_target_pairs={{0,12},{4,8},{8,4},{12,0},{1,13},{5,9},{9,5},{13,1},{2,14},{6,10},... | collective-permute-start | bytes 1081352 | tf_op jit(solution)/shard_map/ppermute | solution.py:289
  37.0 4.3 %collective-permute-start.2 = (f32[2,2,32,128]{3,2,1,0:T(8,128)S(1)}, f32[2,2,32,128]{3,2,1,0:T(8,128)S(1)}, u32[]{:S(2)}, u32[]{:S(2)}) collective-permute-start(f32[2,2,32,128]{3,2,1,0:T(8,128)S(1)} %project.5), channel_id=1, source_target_pairs={{0,16},{16,0},{1,17},{17,1},{2,18},{18,2},{3,19},{19,3},{4,20},{20... | collective-permute-start | bytes 196616 | tf_op jit(solution)/shard_map/ppermute | solution.py:296
  41.3 6.9 %collective-permute-start.5 = (f32[2,4,32,128]{3,2,1,0:T(8,128)S(1)}, f32[2,4,32,128]{3,2,1,0:T(8,128)S(1)}, u32[]{:S(2)}, u32[]{:S(2)}) collective-permute-start(f32[2,4,32,128]{3,2,1,0:T(8,128)S(1)} %join.1.refs_0_), channel_id=1, source_target_pairs={{0,1},{1,0},{2,3},{3,2},{4,5},{5,4},{6,7},{7,6},{8,9},{9,8},{10,11... | collective-permute-start | bytes 393224 | tf_op jit(solution)/shard_map/ppermute | solution.py:304
  42.0 4.4 %collective-permute-start.7 = (f32[2,2,32,128]{3,2,1,0:T(8,128)S(1)}, f32[2,2,32,128]{3,2,1,0:T(8,128)S(1)}, u32[]{:S(2)}, u32[]{:S(2)}) collective-permute-start(f32[2,2,32,128]{3,2,1,0:T(8,128)S(1)} %project.7), channel_id=1, source_target_pairs={{0,17},{1,16},{16,1},{17,0},{2,19},{3,18},{18,3},{19,2},{4,21},{5,... | collective-permute-start | bytes 196616 | tf_op jit(solution)/shard_map/ppermute | solution.py:300
  43.9 4.3 %collective-permute-start.6 = (f32[2,2,32,128]{3,2,1,0:T(8,128)S(1)}, f32[2,2,32,128]{3,2,1,0:T(8,128)S(1)}, u32[]{:S(2)}, u32[]{:S(2)}) collective-permute-start(f32[2,2,32,128]{3,2,1,0:T(8,128)S(1)} %project.7), channel_id=1, source_target_pairs={{0,16},{1,17},{16,0},{17,1},{2,18},{3,19},{18,2},{19,3},{4,20},{5,... | collective-permute-start | bytes 196616 | tf_op jit(solution)/shard_map/ppermute | solution.py:300
  48.2 3.7 %collective-permute-start.8 = (f32[6,128]{1,0:T(8,128)S(1)}, f32[6,128]{1,0:T(8,128)S(1)}, u32[]{:S(2)}, u32[]{:S(2)}) collective-permute-start(f32[6,128]{1,0:T(8,128)S(1)} %get-tuple-element.22), channel_id=1, source_target_pairs={{0,2},{2,0},{1,3},{3,1},{4,6},{6,4},{5,7},{7,5},{8,10},{10,8},{9,1... | collective-permute-start | bytes 9224 | tf_op jit(solution)/shard_map/ppermute | solution.py:309
where the time goes:
time: 52.7 us; the launch traced here: 52.5 us
  waiting for transfers between devices  32.7 us (62%)
  starting transfers between devices  13.1 us (25%)
  Pallas kernels  6.05 us (11%)
  other arithmetic  0.6 us (1%)
    ppermute x1, waiting for transfers between devices, shards(): lax.ppermute(sent_rows[e - 1], 'parts', shifted((parts,), (e,)))  14.9 us
    ppermute x3, waiting for transfers between devices, shards(): slots[j] = lax.ppermute(sent_slots[j - 1], 'shard', to)  10.4 us
    ppermute x3, starting transfers between devices, shards(): slots[j] = lax.ppermute(sent_slots[j - 1], 'shard', to)  4.39 us
    ppermute x2, waiting for transfers between devices, shards(): lax.ppermute(block, ('parts', 'sub'), shifted((parts, subs), (parts - e,...  3.98 us
    ppermute x1, starting transfers between devices, shards(): lax.ppermute(sent_rows[e - 1], 'parts', shifted((parts,), (e,)))  3.06 us
    pallas_call x4, Pallas kernels, project(): pl.pallas_call(functools.partial(project_kernel, len(slots), wide_out), o...  2.37 us
    ppermute x2, starting transfers between devices, shards(): lax.ppermute(block, ('parts', 'sub'), shifted((parts, subs), (parts - e,...  2.19 us
    ppermute x1, waiting for transfers between devices, shards(): out = out + lax.ppermute(blocks[e], 'layer', shifted((layers,), (e,)))  2.12 us
  transfers between devices with their start and end apart: 9, of which 6 were waited for; matrix products, arithmetic and copies ran while one was open for 0% of the time, Pallas kernels for 8%

commit v1 on v0

--- a/solution.py
+++ b/solution.py
@@ -33,8 +33,12 @@
 
 
 def slot_groups(n):
-    late = list(range(max(1, n // 2), n))
+    late = [n // 2] if n > 1 else []
     return [j for j in range(n) if j not in late], late
+
+
+def start_order(n):
+    return list(range(n - 1, n // 2 - 1, -1)) + list(range(1, n // 2))
 
 
 def start_tables(query_hbm, pairs_hbm, query_row, pairs, sem):
@@ -284,7 +288,7 @@
     for e in range(1, parts):
         rows.append(lax.ppermute(sent_rows[e - 1], "parts", shifted((parts,), (e,))))
     slots = [None] * shard_count
-    for j in late[::-1] + early[1:]:
+    for j in start_order(shard_count):
         to = [(i, dest(i, j, shard_count)) for i in range(shard_count)]
         slots[j] = lax.ppermute(sent_slots[j - 1], "shard", to)
     own_rows, slots[0], weights = make_own(early + late, *args)

time: 52.7 us -> 51.9 us (0.985)
    ppermute x3, waiting for transfers between devices: 10.4 us -> 16.3 us  [shards(): slots[j] = lax.ppermute(sent_slots[j - 1], 'shard', to)]
    ppermute x1, waiting for transfers between devices: 14.9 us -> 10.5 us  [shards(): lax.ppermute(sent_rows[e - 1], 'parts', shifted((parts,), (e,)))]
    ppermute x2, waiting for transfers between devices: 3.98 us -> 3.19 us  [shards(): lax.ppermute(block, ('parts', 'sub'), shifted((parts, subs), (parts - e,...]
    ppermute x1, waiting for transfers between devices: 1.3 us -> 0.51 us  [shards(): lax.ppermute(block, 'parts', shifted((parts,), (parts - e,)))]
  transfers between devices with their start and end apart: 9 -> 9, of which waited for: 6 -> 8; matrix products, arithmetic and copies ran while one was open for 0% -> 0% of each run, Pallas kernels for 8% -> 8%
where the time goes in v1:
time: 51.9 us; the launch traced here: 51.7 us
  waiting for transfers between devices  32.5 us (63%)
  starting transfers between devices  12.6 us (24%)
  Pallas kernels  5.94 us (11%)
  other arithmetic  0.6 us (1%)
    ppermute x3, waiting for transfers between devices, shards(): slots[j] = lax.ppermute(sent_slots[j - 1], 'shard', to)  16.3 us
    ppermute x1, waiting for transfers between devices, shards(): lax.ppermute(sent_rows[e - 1], 'parts', shifted((parts,), (e,)))  10.5 us
    ppermute x3, starting transfers between devices, shards(): slots[j] = lax.ppermute(sent_slots[j - 1], 'shard', to)  4.17 us
    ppermute x2, waiting for transfers between devices, shards(): lax.ppermute(block, ('parts', 'sub'), shifted((parts, subs), (parts - e,...  3.19 us
    ppermute x1, starting transfers between devices, shards(): lax.ppermute(sent_rows[e - 1], 'parts', shifted((parts,), (e,)))  3.06 us
    pallas_call x4, Pallas kernels, project(): pl.pallas_call(functools.partial(project_kernel, len(slots), wide_out), o...  2.26 us
    ppermute x1, waiting for transfers between devices, shards(): out = out + lax.ppermute(blocks[e], 'layer', shifted((layers,), (e,)))  2.12 us
    ppermute x2, starting transfers between devices, shards(): lax.ppermute(block, ('parts', 'sub'), shifted((parts, subs), (parts - e,...  1.92 us
  transfers between devices with their start and end apart: 9, of which 8 were waited for; matrix products, arithmetic and copies ran while one was open for 0% of the time, Pallas kernels for 8%

profile of v1, /device:TPU:0, one launch (start us, length us, event | category | flops | bytes accessed | tf_op | source)
XLA Modules:
  0.0 51.7 jit_solution(10023396644775650620)
XLA Ops:
  0.0 1.7 %make_sends.1 = (bf16[32,5632]{1,0:T(8,128)(2,1)S(1)}, bf16[32,5632]{1,0:T(8,128)(2,1)S(1)}, bf16[32,5632]{1,0:T(8,128)(2,1)S(1)}, bf16[128,5632]{1,0:T(8,128)(2,1)S(1)}) custom-call(s32[12]{0:T(128)} %query_hbm.3, s32[2,4,12]{2,1,0:T(4,128)} %pairs_hbm.3, bf16[1,128,7168]{2,1,0:T(8,128)(2,1)} %act.3, bf16[1,128,4096]{2,1,0:T(8,128)(2,1)} %grad.3, ...), custom_call_target="tpu_custom_call" | custom-call | tf_op jit(solution)/shard_map/make_sends/pallas_call | solution.py:110
  1.7 3.1 %collective-permute-start.2 = (bf16[128,5632]{1,0:T(8,128)(2,1)S(1)}, bf16[128,5632]{1,0:T(8,128)(2,1)S(1)}, u32[]{:S(2)}, u32[]{:S(2)}) collective-permute-start(bf16[128,5632]{1,0:T(8,128)(2,1)S(1)} %get-tuple-element.19), channel_id=1, source_target_pairs={{0,16},{16,0},{1,17},{17,1},{2,18},{18,2},{3,19},{19,3},{4,20},{20... | collective-permute-start | bytes 4325384 | tf_op jit(solution)/shard_map/ppermute | solution.py:289
  4.8 1.6 %collective-permute-start = (bf16[32,5632]{1,0:T(8,128)(2,1)S(1)}, bf16[32,5632]{1,0:T(8,128)(2,1)S(1)}, u32[]{:S(2)}, u32[]{:S(2)}) collective-permute-start(bf16[32,5632]{1,0:T(8,128)(2,1)S(1)} %get-tuple-element.16), channel_id=1, source_target_pairs={{0,4},{4,0},{8,12},{12,8},{1,5},{5,1},{9,13},{13,9},{2,6},{6,2},{1... | collective-permute-start | bytes 1081352 | tf_op jit(solution)/shard_map/ppermute | solution.py:293
  6.4 2.5 %collective-permute-start.1 = (bf16[32,5632]{1,0:T(8,128)(2,1)S(1)}, bf16[32,5632]{1,0:T(8,128)(2,1)S(1)}, u32[]{:S(2)}, u32[]{:S(2)}) collective-permute-start(bf16[32,5632]{1,0:T(8,128)(2,1)S(1)} %get-tuple-element.17), channel_id=1, source_target_pairs={{0,12},{4,8},{8,4},{12,0},{1,13},{5,9},{9,5},{13,1},{2,14},{6,10},... | collective-permute-start | bytes 1081352 | tf_op jit(solution)/shard_map/ppermute | solution.py:293
  8.8 0.1 collective-permute-start.4
  9.0 1.9 %make_own.1 = (bf16[128,5632]{1,0:T(8,128)(2,1)S(1)}, bf16[32,5632]{1,0:T(8,128)(2,1)S(1)}, f32[2,4,6,128]{3,2,1,0:T(8,128)S(1)}) custom-call(s32[12]{0:T(128)} %query_hbm.3, s32[2,4,12]{2,1,0:T(4,128)} %pairs_hbm.3, bf16[1,128,7168]{2,1,0:T(8,128)(2,1)} %act.3, bf16[1,128,4096]{2,1,0:T(8,128)(2,1)} %grad.3, bf16[1,3,32,7168]{3,2,1,0:T(8,128)(2,1)} %factor_in.3, ...), custom_call_target="tpu_custom_call" | custom-call | tf_op jit(solution)/shard_map/make_own/pallas_call | solution.py:175
  10.9 4.3 %collective-permute-done.refs_1_ = bf16[32,5632]{1,0:T(8,128)(2,1)S(1)} collective-permute-done((bf16[32,5632]{1,0:T(8,128)(2,1)S(1)}, bf16[32,5632]{1,0:T(8,128)(2,1)S(1)}, u32[]{:S(2)}, u32[]{:S(2)}) %collective-permute-start) | collective-permute-done | bytes 360480 | tf_op jit(solution)/shard_map/ppermute | solution.py:293
  15.2 10.8 %collective-permute-done.1.refs_2_ = bf16[32,5632]{1,0:T(8,128)(2,1)S(1)} collective-permute-done((bf16[32,5632]{1,0:T(8,128)(2,1)S(1)}, bf16[32,5632]{1,0:T(8,128)(2,1)S(1)}, u32[]{:S(2)}, u32[]{:S(2)}) %collective-permute-start.1) | collective-permute-done | bytes 360480 | tf_op jit(solution)/shard_map/ppermute | solution.py:293
  25.9 10.5 %collective-permute-done.2.refs_3_.refs_1_ = bf16[128,5632]{1,0:T(8,128)(2,1)S(1)} collective-permute-done((bf16[128,5632]{1,0:T(8,128)(2,1)S(1)}, bf16[128,5632]{1,0:T(8,128)(2,1)S(1)}, u32[]{:S(2)}, u32[]{:S(2)}) %collective-permute-start.2) | collective-permute-done | bytes 1441824 | tf_op jit(solution)/shard_map/ppermute | solution.py:289
  36.4 0.6 %project.5 = f32[2,3,32,128]{3,2,1,0:T(8,128)S(1)} custom-call(bf16[32,5632]{1,0:T(8,128)(2,1)S(1)} %get-tuple-element.15.refs_0_, bf16[32,5632]{1,0:T(8,128)(2,1)S(1)} %collective-permute-done.refs_1_, bf16[32,5632]{1,0:T(8,128)(2,1)S(1)} %collective-permute-done.1.refs_2_, bf16[128,5632]{1,0:T(8,128)(2,1)S(1)} %collective-permute-done.2.refs_3_.refs_1_), custom_call_target="tpu_custom_call" | custom-call | flops 138412032 | bytes 2523136 | tf_op jit(solution)/shard_map/project/pallas_call | solution.py:205
  37.0 1.8 %collective-permute-start.3 = (f32[2,3,32,128]{3,2,1,0:T(8,128)S(1)}, f32[2,3,32,128]{3,2,1,0:T(8,128)S(1)}, u32[]{:S(2)}, u32[]{:S(2)}) collective-permute-start(f32[2,3,32,128]{3,2,1,0:T(8,128)S(1)} %project.5), channel_id=1, source_target_pairs={{0,16},{16,0},{1,17},{17,1},{2,18},{18,2},{3,19},{19,3},{4,20},{20... | collective-permute-start | bytes 294920 | tf_op jit(solution)/shard_map/ppermute | solution.py:300
  38.8 1.2 %collective-permute-done.4.refs_0_ = bf16[32,5632]{1,0:T(8,128)(2,1)S(1)} collective-permute-done((bf16[32,5632]{1,0:T(8,128)(2,1)S(1)}, bf16[32,5632]{1,0:T(8,128)(2,1)S(1)}, u32[]{:S(2)}, u32[]{:S(2)}) %collective-permute-start.4) | collective-permute-done | bytes 360480 | tf_op jit(solution)/shard_map/ppermute | solution.py:293
  40.0 0.5 %project.6.refs_2_ = f32[2,1,32,128]{3,2,1,0:T(8,128)S(1)} custom-call(bf16[32,5632]{1,0:T(8,128)(2,1)S(1)} %collective-permute-done.4.refs_0_, bf16[128,5632]{1,0:T(8,128)(2,1)S(1)} %get-tuple-element.18.refs_3_.refs_1_), custom_call_target="tpu_custom_call" | custom-call | flops 46137344 | bytes 1802240 | tf_op jit(solution)/shard_map/project/pallas_call | solution.py:205
  40.5 0.6 %project.4.refs_0_ = f32[2,3,32,128]{3,2,1,0:T(8,128)S(1)} custom-call(bf16[32,5632]{1,0:T(8,128)(2,1)S(1)} %get-tuple-element.15.refs_0_, bf16[32,5632]{1,0:T(8,128)(2,1)S(1)} %collective-permute-done.refs_1_, bf16[32,5632]{1,0:T(8,128)(2,1)S(1)} %collective-permute-done.1.refs_2_, bf16[128,5632]{1,0:T(8,128)(2,1)S(1)} %get-tuple-element.18.refs_3_.refs_1_), custom_call_target="tpu_custom_call" | custom-call | flops 138412032 | bytes 2523136 | tf_op jit(solution)/shard_map/project/pallas_call | solution.py:205
  41.1 0.5 collective-permute-done.3.refs_1_
  41.7 0.1 collective-permute-start.5
  41.7 0.5 %project.7 = f32[2,1,32,128]{3,2,1,0:T(8,128)S(1)} custom-call(bf16[32,5632]{1,0:T(8,128)(2,1)S(1)} %collective-permute-done.4.refs_0_, bf16[128,5632]{1,0:T(8,128)(2,1)S(1)} %collective-permute-done.2.refs_3_.refs_1_), custom_call_target="tpu_custom_call" | custom-call | flops 46137344 | bytes 1802240 | tf_op jit(solution)/shard_map/project/pallas_call | solution.py:205
  42.3 1.8 %collective-permute-start.6 = (f32[2,1,32,128]{3,2,1,0:T(8,128)S(1)}, f32[2,1,32,128]{3,2,1,0:T(8,128)S(1)}, u32[]{:S(2)}, u32[]{:S(2)}) collective-permute-start(f32[2,1,32,128]{3,2,1,0:T(8,128)S(1)} %project.7), channel_id=1, source_target_pairs={{0,16},{1,17},{16,0},{17,1},{2,18},{3,19},{18,2},{19,3},{4,20},{5,... | collective-permute-start | bytes 98312 | tf_op jit(solution)/shard_map/ppermute | solution.py:304
  44.0 0.1 collective-permute-start.7
  44.2 2.0 %collective-permute-done.6.refs_2_ = f32[2,1,32,128]{3,2,1,0:T(8,128)S(1)} collective-permute-done((f32[2,1,32,128]{3,2,1,0:T(8,128)S(1)}, f32[2,1,32,128]{3,2,1,0:T(8,128)S(1)}, u32[]{:S(2)}, u32[]{:S(2)}) %collective-permute-start.6) | collective-permute-done | bytes 32800 | tf_op jit(solution)/shard_map/ppermute | solution.py:304
  46.2 1.2 %collective-permute-done.7.refs_3_ = f32[2,1,32,128]{3,2,1,0:T(8,128)S(1)} collective-permute-done((f32[2,1,32,128]{3,2,1,0:T(8,128)S(1)}, f32[2,1,32,128]{3,2,1,0:T(8,128)S(1)}, u32[]{:S(2)}, u32[]{:S(2)}) %collective-permute-start.7) | collective-permute-done | bytes 32800 | tf_op jit(solution)/shard_map/ppermute | solution.py:304
  47.4 0.0 collective-permute-done.5.refs_1_
  47.4 1.5 %collective-permute-start.8 = (f32[6,128]{1,0:T(8,128)S(1)}, f32[6,128]{1,0:T(8,128)S(1)}, u32[]{:S(2)}, u32[]{:S(2)}) collective-permute-start(f32[6,128]{1,0:T(8,128)S(1)} %get-tuple-element.22), channel_id=1, source_target_pairs={{0,2},{2,0},{1,3},{3,1},{4,6},{6,4},{5,7},{7,5},{8,10},{10,8},{9,1... | collective-permute-start | bytes 9224 | tf_op jit(solution)/shard_map/ppermute | solution.py:313
  49.0 2.1 %collective-permute-done.8 = f32[6,128]{1,0:T(8,128)S(1)} collective-permute-done((f32[6,128]{1,0:T(8,128)S(1)}, f32[6,128]{1,0:T(8,128)S(1)}, u32[]{:S(2)}, u32[]{:S(2)}) %collective-permute-start.8) | collective-permute-done | bytes 3104 | tf_op jit(solution)/shard_map/ppermute | solution.py:313
  51.1 0.6 %add_bitcast_fusion = f32[128,6]{0,1:T(8,128)} fusion(f32[6,128]{1,0:T(8,128)S(1)} %get-tuple-element.21, f32[6,128]{1,0:T(8,128)S(1)} %collective-permute-done.8), kind=kLoop, calls=%fused_computation | loop fusion | flops 768 | bytes 9216 | tf_op jit(solution)/shard_map/transpose | solution.py:314
  (2 shorter events, 0.0 us)
Async XLA Ops:
  1.7 34.6 %collective-permute-start.2 = (bf16[128,5632]{1,0:T(8,128)(2,1)S(1)}, bf16[128,5632]{1,0:T(8,128)(2,1)S(1)}, u32[]{:S(2)}, u32[]{:S(2)}) collective-permute-start(bf16[128,5632]{1,0:T(8,128)(2,1)S(1)} %get-tuple-element.19), channel_id=1, source_target_pairs={{0,16},{16,0},{1,17},{17,1},{2,18},{18,2},{3,19},{19,3},{4,20},{20... | collective-permute-start | bytes 4325384 | tf_op jit(solution)/shard_map/ppermute | solution.py:289
  4.8 10.4 %collective-permute-start = (bf16[32,5632]{1,0:T(8,128)(2,1)S(1)}, bf16[32,5632]{1,0:T(8,128)(2,1)S(1)}, u32[]{:S(2)}, u32[]{:S(2)}) collective-permute-start(bf16[32,5632]{1,0:T(8,128)(2,1)S(1)} %get-tuple-element.16), channel_id=1, source_target_pairs={{0,4},{4,0},{8,12},{12,8},{1,5},{5,1},{9,13},{13,9},{2,6},{6,2},{1... | collective-permute-start | bytes 1081352 | tf_op jit(solution)/shard_map/ppermute | solution.py:293
  6.4 19.6 %collective-permute-start.1 = (bf16[32,5632]{1,0:T(8,128)(2,1)S(1)}, bf16[32,5632]{1,0:T(8,128)(2,1)S(1)}, u32[]{:S(2)}, u32[]{:S(2)}) collective-permute-start(bf16[32,5632]{1,0:T(8,128)(2,1)S(1)} %get-tuple-element.17), channel_id=1, source_target_pairs={{0,12},{4,8},{8,4},{12,0},{1,13},{5,9},{9,5},{13,1},{2,14},{6,10},... | collective-permute-start | bytes 1081352 | tf_op jit(solution)/shard_map/ppermute | solution.py:293
  8.8 31.1 %collective-permute-start.4 = (bf16[32,5632]{1,0:T(8,128)(2,1)S(1)}, bf16[32,5632]{1,0:T(8,128)(2,1)S(1)}, u32[]{:S(2)}, u32[]{:S(2)}) collective-permute-start(bf16[32,5632]{1,0:T(8,128)(2,1)S(1)} %get-tuple-element.20), channel_id=1, source_target_pairs={{0,8},{4,12},{8,0},{12,4},{1,9},{5,13},{9,1},{13,5},{2,10},{6,14},... | collective-permute-start | bytes 1081352 | tf_op jit(solution)/shard_map/ppermute | solution.py:293
  37.0 4.7 %collective-permute-start.3 = (f32[2,3,32,128]{3,2,1,0:T(8,128)S(1)}, f32[2,3,32,128]{3,2,1,0:T(8,128)S(1)}, u32[]{:S(2)}, u32[]{:S(2)}) collective-permute-start(f32[2,3,32,128]{3,2,1,0:T(8,128)S(1)} %project.5), channel_id=1, source_target_pairs={{0,16},{16,0},{1,17},{17,1},{2,18},{18,2},{3,19},{19,3},{4,20},{20... | collective-permute-start | bytes 294920 | tf_op jit(solution)/shard_map/ppermute | solution.py:300
  41.7 5.7 %collective-permute-start.5 = (f32[2,4,32,128]{3,2,1,0:T(8,128)S(1)}, f32[2,4,32,128]{3,2,1,0:T(8,128)S(1)}, u32[]{:S(2)}, u32[]{:S(2)}) collective-permute-start(f32[2,4,32,128]{3,2,1,0:T(8,128)S(1)} %join.1.refs_0_), channel_id=1, source_target_pairs={{0,1},{1,0},{2,3},{3,2},{4,5},{5,4},{6,7},{7,6},{8,9},{9,8},{10,11... | collective-permute-start | bytes 393224 | tf_op jit(solution)/shard_map/ppermute | solution.py:308
  42.3 3.9 %collective-permute-start.6 = (f32[2,1,32,128]{3,2,1,0:T(8,128)S(1)}, f32[2,1,32,128]{3,2,1,0:T(8,128)S(1)}, u32[]{:S(2)}, u32[]{:S(2)}) collective-permute-start(f32[2,1,32,128]{3,2,1,0:T(8,128)S(1)} %project.7), channel_id=1, source_target_pairs={{0,16},{1,17},{16,0},{17,1},{2,18},{3,19},{18,2},{19,3},{4,20},{5,... | collective-permute-start | bytes 98312 | tf_op jit(solution)/shard_map/ppermute | solution.py:304
  44.0 3.3 %collective-permute-start.7 = (f32[2,1,32,128]{3,2,1,0:T(8,128)S(1)}, f32[2,1,32,128]{3,2,1,0:T(8,128)S(1)}, u32[]{:S(2)}, u32[]{:S(2)}) collective-permute-start(f32[2,1,32,128]{3,2,1,0:T(8,128)S(1)} %project.7), channel_id=1, source_target_pairs={{0,17},{1,16},{16,1},{17,0},{2,19},{3,18},{18,3},{19,2},{4,21},{5,... | collective-permute-start | bytes 98312 | tf_op jit(solution)/shard_map/ppermute | solution.py:304
  47.4 3.7 %collective-permute-start.8 = (f32[6,128]{1,0:T(8,128)S(1)}, f32[6,128]{1,0:T(8,128)S(1)}, u32[]{:S(2)}, u32[]{:S(2)}) collective-permute-start(f32[6,128]{1,0:T(8,128)S(1)} %get-tuple-element.22), channel_id=1, source_target_pairs={{0,2},{2,0},{1,3},{3,1},{4,6},{6,4},{5,7},{7,5},{8,10},{10,8},{9,1... | collective-permute-start | bytes 9224 | tf_op jit(solution)/shard_map/ppermute | solution.py:313

commit v2 on v1

--- a/solution.py
+++ b/solution.py
@@ -124,30 +124,29 @@
     return sent[: shard_count - 1], sent[shard_count - 1 :]
 
 
-def own_kernel(parts, order, query_hbm, pairs_hbm, act, grad, factor_in, factor_out, rows, slot, weights, *scratch):
-    query_row, pairs, sem, table_sem = scratch
+def own_kernel(parts, order, query_hbm, pairs_hbm, act, grad, factor_in, factor_out, rows, *refs):
+    slots, (weights, query_row, pairs, sem, table_sem) = refs[:parts], refs[parts:]
     tables = start_tables(query_hbm, pairs_hbm, query_row, pairs, table_sem)
     my_part, my_shard, my_layer = lax.axis_index("parts"), lax.axis_index("shard"), lax.axis_index("layer")
     layers, shard_count = lax.axis_size("layer"), lax.axis_size("shard")
     per_owner, tokens = factor_out.shape[1], rows.shape[0]
     wide_out, wide_in = grad.shape[2] // parts, act.shape[2] // parts
-    span_out, span_in = span(my_part, wide_out), span(my_part, wide_in)
     to_out, to_in = pl.ds(0, wide_out), pl.ds(wide_out, wide_in)
-    copies = [
-        pltpu.make_async_copy(grad.at[0, :, span_out], rows.at[:, to_out], sem.at[0]),
-        pltpu.make_async_copy(act.at[0, :, span_in], rows.at[:, to_in], sem.at[1]),
-    ]
-    for copy in copies:
-        copy.start()
+    copies = []
+
+    def start(piece, target):
+        copies.append(pltpu.make_async_copy(piece, target, sem.at[len(copies)]))
+        copies[-1].start()
+
+    start(grad.at[0, :, span(my_part, wide_out)], rows.at[:, to_out])
+    start(act.at[0, :, span(my_part, wide_in)], rows.at[:, to_in])
     for table in tables:
         table.wait()
     (row,) = pick_rows(query_row, pairs, per_owner, [my_shard])
-    copies += [
-        pltpu.make_async_copy(factor_out.at[0, row, :, span_out], slot.at[:, to_out], sem.at[2]),
-        pltpu.make_async_copy(factor_in.at[0, row, :, span_in], slot.at[:, to_in], sem.at[3]),
-    ]
-    for copy in copies[2:]:
-        copy.start()
+    for e, slot in enumerate(slots):
+        part = wrap(my_part + e, parts)
+        start(factor_out.at[0, row, :, span(part, wide_out)], slot.at[:, to_out])
+        start(factor_in.at[0, row, :, span(part, wide_in)], slot.at[:, to_in])
     wide = query_row.shape[0] // layers
     for e in range(layers):
         layer = wrap(my_layer + e, layers)
@@ -169,7 +168,7 @@
     wide = (grad.shape[2] + act.shape[2]) // parts
     shapes = [
         pltpu.VMEM((tokens, wide), act.dtype),
-        pltpu.VMEM((rank, wide), act.dtype),
+        *[pltpu.VMEM((rank, wide), act.dtype)] * parts,
         pltpu.VMEM((layers, len(order), query_row.shape[0] // layers, tokens), jnp.float32),
     ]
     return pl.pallas_call(
@@ -177,98 +176,99 @@
         out_shape=shapes,
         in_specs=[pl.BlockSpec(memory_space=pltpu.HBM)] * 6,
         out_specs=[pl.BlockSpec(memory_space=pltpu.VMEM)] * len(shapes),
-        scratch_shapes=table_scratch(query_row, pairs) + [pltpu.SemaphoreType.DMA((4,)), pltpu.SemaphoreType.DMA((2,))],
+        scratch_shapes=table_scratch(query_row, pairs)
+        + [pltpu.SemaphoreType.DMA((2 + 2 * parts,)), pltpu.SemaphoreType.DMA((2,))],
         compiler_params=pltpu.CompilerParams(vmem_limit_bytes=2**22),
         name="make_own",
     )(query_row, pairs, act, grad, factor_in, factor_out)
 
 
+def vmem_call(kernel, shapes, inputs, flops=0):
+    vmem = pl.BlockSpec(memory_space=pltpu.VMEM)
+    inputs = [pltpu.with_memory_space_constraint(x, pltpu.VMEM) for x in inputs]
+    read = sum(x.size * x.dtype.itemsize for x in inputs)
+    return pl.pallas_call(
+        kernel,
+        out_shape=[pltpu.VMEM(shape, jnp.float32) for shape in shapes],
+        in_specs=[vmem] * len(inputs),
+        out_specs=[vmem] * len(shapes),
+        compiler_params=pltpu.CompilerParams(vmem_limit_bytes=2**23),
+        cost_estimate=pl.CostEstimate(flops=flops, bytes_accessed=read, transcendentals=0),
+    )(*inputs)
+
+
 def project_kernel(slot_count, wide_out, *refs):
-    slots, rest = refs[:slot_count], refs[slot_count:]
-    blocks, outs = rest[: len(rest) // 2], rest[len(rest) // 2 :]
-    dims = (((1,), (1,)), ((), ()))
+    slots, rows, out = refs[:slot_count], refs[slot_count], refs[-1]
     rank, wide = slots[0].shape
     for which, (low, high) in enumerate(((0, wide_out), (wide_out, wide))):
         left = jnp.concatenate([slot[:, low:high] for slot in slots], axis=0)
-        for block, out in zip(blocks, outs):
-            proj = lax.dot_general(left, block[:, low:high], dims, preferred_element_type=jnp.float32)
-            for j in range(slot_count):
-                out[which, j] = proj[j * rank : (j + 1) * rank]
-
-
-def project(slots, blocks, wide_out):
-    vmem = pl.BlockSpec(memory_space=pltpu.VMEM)
-    (rank, wide), tokens = slots[0].shape, blocks[0].shape[0]
-    inputs = [pltpu.with_memory_space_constraint(x, pltpu.VMEM) for x in (*slots, *blocks)]
-    flops = 2 * len(slots) * rank * len(blocks) * tokens * wide
-    read = 2 * wide * (len(slots) * rank + len(blocks) * tokens)
-    return pl.pallas_call(
-        functools.partial(project_kernel, len(slots), wide_out),
-        out_shape=[pltpu.VMEM((2, len(slots), rank, tokens), jnp.float32)] * len(blocks),
-        in_specs=[vmem] * len(inputs),
-        out_specs=[vmem] * len(blocks),
-        compiler_params=pltpu.CompilerParams(vmem_limit_bytes=2**23),
-        cost_estimate=pl.CostEstimate(flops=flops, bytes_accessed=read, transcendentals=0),
-        name="project",
-    )(*inputs)
-
-
-def join_kernel(*refs):
-    early, late, out = refs[:-2], refs[-2], refs[-1]
-    total = early[0][...]
-    for piece in early[1:]:
+        proj = lax.dot_general(left, rows[:, low:high], (((1,), (1,)), ((), ())), preferred_element_type=jnp.float32)
+        for j in range(slot_count):
+            out[which, j] = proj[j * rank : (j + 1) * rank]
+
+
+def project(slots, rows, wide_out):
+    (rank, wide), tokens = slots[0].shape, rows.shape[0]
+    kernel = functools.partial(project_kernel, len(slots), wide_out)
+    flops = 2 * len(slots) * rank * tokens * wide
+    return vmem_call(kernel, [(2, len(slots), rank, tokens)], [*slots, rows], flops)[0]
+
+
+def local_kernel(wide_out, *refs):
+    count = len(refs) // 2
+    slots, rows, out = refs[:count], refs[count:-1], refs[-1]
+    for which, (low, high) in enumerate(((0, wide_out), (wide_out, slots[0].shape[1]))):
+        total = None
+        for slot, block in zip(slots, rows):
+            proj = lax.dot_general(
+                slot[:, low:high], block[:, low:high], (((1,), (1,)), ((), ())), preferred_element_type=jnp.float32
+            )
+            total = proj if total is None else total + proj
+        out[which, 0] = total
+
+
+def project_local(slots, rows, wide_out):
+    (rank, wide), tokens = slots[0].shape, rows[0].shape[0]
+    kernel = functools.partial(local_kernel, wide_out)
+    return vmem_call(kernel, [(2, 1, rank, tokens)], [*slots, *rows], 2 * len(slots) * rank * tokens * wide)[0]
+
+
+def join_kernel(counts, *refs):
+    pieces, out = list(refs[:-1]), refs[-1]
+    done = 0
+    for count in counts:
+        group = [pieces.pop(0) for _ in range(count)]
+        total = group[0][...]
+        for piece in group[1:]:
+            total = total + piece[...]
+        out[:, done : done + total.shape[1]] = total
+        done += total.shape[1]
+
+
+def join(groups):
+    slots = sum(group[0].shape[1] for group in groups)
+    kernel = functools.partial(join_kernel, [len(group) for group in groups])
+    shape = (2, slots, *groups[0][0].shape[2:])
+    return vmem_call(kernel, [shape], [piece for group in groups for piece in group])[0]
+
+
+def score_kernel(weights, *refs):
+    layers, slots = weights.shape[:2]
+    pieces, outs = refs[:-layers], refs[-layers:]
+    total = pieces[0][...]
+    for piece in pieces[1:]:
         total = total + piece[...]
-    out[:, : total.shape[1]] = total
-    out[:, total.shape[1] :] = late[...]
-
-
-def join(early, late):
-    vmem = pl.BlockSpec(memory_space=pltpu.VMEM)
-    inputs = [pltpu.with_memory_space_constraint(x, pltpu.VMEM) for x in (*early, late)]
-    return pl.pallas_call(
-        join_kernel,
-        out_shape=pltpu.VMEM((2, early[0].shape[1] + late.shape[1], *late.shape[2:]), jnp.float32),
-        in_specs=[vmem] * len(inputs),
-        out_specs=vmem,
-        compiler_params=pltpu.CompilerParams(vmem_limit_bytes=2**23),
-        name="join",
-    )(*inputs)
-
-
-def score_kernel(done, whole_count, weights, *refs):
-    layers = weights.shape[0]
-    pieces, outs = refs[:-layers], refs[-layers:]
-    whole, parted = pieces[:whole_count], pieces[whole_count:]
-    total = whole[0][...]
-    for piece in whole[1:]:
-        total = total + piece[...]
-    first, last = total[:, :done], total[:, done:]
-    if parted:
-        more = parted[0][...]
-        for piece in parted[1:]:
-            more = more + piece[...]
-        last = last + more
-    scores = [jnp.sum(t[0, k] * t[1, k], axis=0, keepdims=True) for t in (first, last) for k in range(t.shape[1])]
+    scores = [jnp.sum(total[0, k] * total[1, k], axis=0, keepdims=True) for k in range(slots)]
     for e, out in enumerate(outs):
         block = weights[e, 0] * scores[0]
-        for k in range(1, len(scores)):
+        for k in range(1, slots):
             block = block + weights[e, k] * scores[k]
         out[...] = block
 
 
-def make_scores(weights, whole, parted):
-    layers, count, wide, tokens = weights.shape
-    vmem = pl.BlockSpec(memory_space=pltpu.VMEM)
-    inputs = [pltpu.with_memory_space_constraint(x, pltpu.VMEM) for x in (weights, *whole, *parted)]
-    done = count - (parted[0].shape[1] if parted else 0)
-    return pl.pallas_call(
-        functools.partial(score_kernel, done, len(whole)),
-        out_shape=[pltpu.VMEM((wide, tokens), jnp.float32)] * layers,
-        in_specs=[vmem] * len(inputs),
-        out_specs=[vmem] * layers,
-        compiler_params=pltpu.CompilerParams(vmem_limit_bytes=2**23),
-        name="make_scores",
-    )(*inputs)
+def make_scores(weights, pieces):
+    layers, _, wide, tokens = weights.shape
+    return vmem_call(score_kernel, [(wide, tokens)] * layers, [weights, *pieces])
 
 
 def shards(act_in, grad_out, factor_in, factor_out, query_row, pairs):
@@ -291,22 +291,26 @@
     for j in start_order(shard_count):
         to = [(i, dest(i, j, shard_count)) for i in range(shard_count)]
         slots[j] = lax.ppermute(sent_slots[j - 1], "shard", to)
-    own_rows, slots[0], weights = make_own(early + late, *args)
-
-    early_own = project([slots[j] for j in early], [own_rows], wide_out)
-    early_rest = project([slots[j] for j in early], rows, wide_out) if rows else []
-    early_got, late_got = [], []
-    for e, block in enumerate(early_rest, 1):
-        early_got.append(lax.ppermute(block, "parts", shifted((parts,), (parts - e,))))
-    late_rest = project([slots[j] for j in late], rows, wide_out) if rows else []
-    for e, block in enumerate(late_rest, 1):
-        for f in range(subs):
-            late_got.append(lax.ppermute(block, ("parts", "sub"), shifted((parts, subs), (parts - e, f))))
-    (late_own,) = project([slots[j] for j in late], [own_rows], wide_out)
-    whole = [join(list(early_own) + early_got, late_own)]
+    own_rows, *own_slots, weights = make_own(early + late, *args)
+
+    groups = [[project_local(own_slots, [own_rows] + list(sent_rows), wide_out)]]
+
+    def sums(numbers):
+        if not numbers:
+            return
+        group = []
+        for e, block in enumerate(rows, 1):
+            part_sums = project([slots[j] for j in numbers], block, wide_out)
+            group.append(lax.ppermute(part_sums, "parts", shifted((parts,), (parts - e,))))
+        group.insert(0, project([slots[j] for j in numbers], own_rows, wide_out))
+        groups.append(group)
+
+    sums(early[1:])
+    sums(late)
+    whole = [join(groups)]
     for f in range(1, subs):
         whole.append(lax.ppermute(whole[0], "sub", shifted((subs,), (f,))))
-    blocks = make_scores(weights, whole, late_got)
+    blocks = make_scores(weights, whole)
 
     out = blocks[0]
     for e in range(1, layers):

time: 51.9 us -> 51.2 us (0.987)
  starting transfers between devices: 12.6 us -> 11.2 us
  Pallas kernels: 5.94 us -> 7.13 us
    ppermute x3 -> x2, waiting for transfers between devices: 3.7 us -> 0.01 us  [sums(): lax.ppermute(part_sums, 'parts', shifted((parts,), (parts - e,)))]
    ppermute x3, waiting for transfers between devices: 16.3 us -> 18.2 us  [shards(): slots[j] = lax.ppermute(sent_slots[j - 1], 'shard', to)]
    ppermute x3 -> x2, starting transfers between devices: 3.73 us -> 2.33 us  [sums(): lax.ppermute(part_sums, 'parts', shifted((parts,), (parts - e,)))]
    ppermute x1, waiting for transfers between devices: 0.01 us -> 1.33 us  [shards(): whole.append(lax.ppermute(whole[0], 'sub', shifted((subs,), (f,))))]
    pallas_call x6 -> x7, Pallas kernels: 2.31 us -> 3.37 us  [vmem_call(): pl.pallas_call(kernel, out_shape=[pltpu.VMEM(shape, jnp.float32) for shap...]
  transfers between devices with their start and end apart: 9 -> 8, of which waited for: 8 -> 6; matrix products, arithmetic and copies ran while one was open for 0% -> 0% of each run, Pallas kernels for 8% -> 10%
where the time goes in v2:
time: 51.2 us; the launch traced here: 51 us
  waiting for transfers between devices  32.1 us (63%)
  starting transfers between devices  11.2 us (22%)
  Pallas kernels  7.13 us (14%)
  other arithmetic  0.6 us (1%)
    ppermute x3, waiting for transfers between devices, shards(): slots[j] = lax.ppermute(sent_slots[j - 1], 'shard', to)  18.2 us
    ppermute x1, waiting for transfers between devices, shards(): lax.ppermute(sent_rows[e - 1], 'parts', shifted((parts,), (e,)))  10.5 us
    ppermute x3, starting transfers between devices, shards(): slots[j] = lax.ppermute(sent_slots[j - 1], 'shard', to)  4.17 us
    pallas_call x7, Pallas kernels, vmem_call(): pl.pallas_call(kernel, out_shape=[pltpu.VMEM(shape, jnp.float32) for shap...  3.37 us
    ppermute x1, starting transfers between devices, shards(): lax.ppermute(sent_rows[e - 1], 'parts', shifted((parts,), (e,)))  3.06 us
    ppermute x2, starting transfers between devices, sums(): lax.ppermute(part_sums, 'parts', shifted((parts,), (parts - e,)))  2.33 us
    ppermute x1, waiting for transfers between devices, shards(): out = out + lax.ppermute(blocks[e], 'layer', shifted((layers,), (e,)))  2.12 us
    pallas_call x1, Pallas kernels, make_own(): pl.pallas_call(functools.partial(own_kernel, parts, tuple(order)), out_sh...  2.03 us
  transfers between devices with their start and end apart: 8, of which 6 were waited for; matrix products, arithmetic and copies ran while one was open for 0% of the time, Pallas kernels for 10%

profile of v2, /device:TPU:0, one launch (start us, length us, event | category | flops | bytes accessed | tf_op | source)
XLA Modules:
  0.0 51.0 jit_solution(8960390251232198453)
XLA Ops:
  0.0 1.7 %make_sends.1 = (bf16[32,5632]{1,0:T(8,128)(2,1)S(1)}, bf16[32,5632]{1,0:T(8,128)(2,1)S(1)}, bf16[32,5632]{1,0:T(8,128)(2,1)S(1)}, bf16[128,5632]{1,0:T(8,128)(2,1)S(1)}) custom-call(s32[12]{0:T(128)} %query_hbm.3, s32[2,4,12]{2,1,0:T(4,128)} %pairs_hbm.3, bf16[1,128,7168]{2,1,0:T(8,128)(2,1)} %act.3, bf16[1,128,4096]{2,1,0:T(8,128)(2,1)} %grad.3, ...), custom_call_target="tpu_custom_call" | custom-call | tf_op jit(solution)/shard_map/make_sends/pallas_call | solution.py:110
  1.7 3.1 %collective-permute-start.2 = (bf16[128,5632]{1,0:T(8,128)(2,1)S(1)}, bf16[128,5632]{1,0:T(8,128)(2,1)S(1)}, u32[]{:S(2)}, u32[]{:S(2)}) collective-permute-start(bf16[128,5632]{1,0:T(8,128)(2,1)S(1)} %get-tuple-element.19.refs_3_), channel_id=1, source_target_pairs={{0,16},{16,0},{1,17},{17,1},{2,18},{18,2},{3,19},{19,3},{4,20},{20... | collective-permute-start | bytes 4325384 | tf_op jit(solution)/shard_map/ppermute | solution.py:289
  4.8 1.6 %collective-permute-start = (bf16[32,5632]{1,0:T(8,128)(2,1)S(1)}, bf16[32,5632]{1,0:T(8,128)(2,1)S(1)}, u32[]{:S(2)}, u32[]{:S(2)}) collective-permute-start(bf16[32,5632]{1,0:T(8,128)(2,1)S(1)} %get-tuple-element.20), channel_id=1, source_target_pairs={{0,4},{4,0},{8,12},{12,8},{1,5},{5,1},{9,13},{13,9},{2,6},{6,2},{1... | collective-permute-start | bytes 1081352 | tf_op jit(solution)/shard_map/ppermute | solution.py:293
  6.4 2.5 %collective-permute-start.1 = (bf16[32,5632]{1,0:T(8,128)(2,1)S(1)}, bf16[32,5632]{1,0:T(8,128)(2,1)S(1)}, u32[]{:S(2)}, u32[]{:S(2)}) collective-permute-start(bf16[32,5632]{1,0:T(8,128)(2,1)S(1)} %get-tuple-element.21), channel_id=1, source_target_pairs={{0,12},{4,8},{8,4},{12,0},{1,13},{5,9},{9,5},{13,1},{2,14},{6,10},... | collective-permute-start | bytes 1081352 | tf_op jit(solution)/shard_map/ppermute | solution.py:293
  8.8 0.1 collective-permute-start.4
  9.0 6.2 %collective-permute-done.refs_0_ = bf16[32,5632]{1,0:T(8,128)(2,1)S(1)} collective-permute-done((bf16[32,5632]{1,0:T(8,128)(2,1)S(1)}, bf16[32,5632]{1,0:T(8,128)(2,1)S(1)}, u32[]{:S(2)}, u32[]{:S(2)}) %collective-permute-start) | collective-permute-done | bytes 360480 | tf_op jit(solution)/shard_map/ppermute | solution.py:293
  15.2 10.8 %collective-permute-done.1.refs_1_ = bf16[32,5632]{1,0:T(8,128)(2,1)S(1)} collective-permute-done((bf16[32,5632]{1,0:T(8,128)(2,1)S(1)}, bf16[32,5632]{1,0:T(8,128)(2,1)S(1)}, u32[]{:S(2)}, u32[]{:S(2)}) %collective-permute-start.1) | collective-permute-done | bytes 360480 | tf_op jit(solution)/shard_map/ppermute | solution.py:293
  25.9 10.5 %collective-permute-done.2.refs_2_.refs_1_ = bf16[128,5632]{1,0:T(8,128)(2,1)S(1)} collective-permute-done((bf16[128,5632]{1,0:T(8,128)(2,1)S(1)}, bf16[128,5632]{1,0:T(8,128)(2,1)S(1)}, u32[]{:S(2)}, u32[]{:S(2)}) %collective-permute-start.2) | collective-permute-done | bytes 1441824 | tf_op jit(solution)/shard_map/ppermute | solution.py:289
  36.4 0.6 %shard_map.66 = f32[2,2,32,128]{3,2,1,0:T(8,128)S(1)} custom-call(bf16[32,5632]{1,0:T(8,128)(2,1)S(1)} %collective-permute-done.refs_0_, bf16[32,5632]{1,0:T(8,128)(2,1)S(1)} %collective-permute-done.1.refs_1_, bf16[128,5632]{1,0:T(8,128)(2,1)S(1)} %collective-permute-done.2.refs_2_.refs_1_), custom_call_target="tpu_custom_call" | custom-call | flops 92274688 | bytes 2162688 | tf_op jit(solution)/shard_map/pallas_call | solution.py:190
  37.0 1.8 %collective-permute-start.3 = (f32[2,2,32,128]{3,2,1,0:T(8,128)S(1)}, f32[2,2,32,128]{3,2,1,0:T(8,128)S(1)}, u32[]{:S(2)}, u32[]{:S(2)}) collective-permute-start(f32[2,2,32,128]{3,2,1,0:T(8,128)S(1)} %shard_map.66), channel_id=1, source_target_pairs={{0,16},{16,0},{1,17},{17,1},{2,18},{18,2},{3,19},{19,3},{4,20},{20... | collective-permute-start | bytes 196616 | tf_op jit(solution)/shard_map/ppermute | solution.py:304
  38.8 1.2 %collective-permute-done.4.refs_0_ = bf16[32,5632]{1,0:T(8,128)(2,1)S(1)} collective-permute-done((bf16[32,5632]{1,0:T(8,128)(2,1)S(1)}, bf16[32,5632]{1,0:T(8,128)(2,1)S(1)}, u32[]{:S(2)}, u32[]{:S(2)}) %collective-permute-start.4) | collective-permute-done | bytes 360480 | tf_op jit(solution)/shard_map/ppermute | solution.py:293
  40.0 0.5 %shard_map.68 = f32[2,1,32,128]{3,2,1,0:T(8,128)S(1)} custom-call(bf16[32,5632]{1,0:T(8,128)(2,1)S(1)} %collective-permute-done.4.refs_0_, bf16[128,5632]{1,0:T(8,128)(2,1)S(1)} %collective-permute-done.2.refs_2_.refs_1_), custom_call_target="tpu_custom_call" | custom-call | flops 46137344 | bytes 1802240 | tf_op jit(solution)/shard_map/pallas_call | solution.py:190
  40.5 0.5 %collective-permute-start.5 = (f32[2,1,32,128]{3,2,1,0:T(8,128)S(1)}, f32[2,1,32,128]{3,2,1,0:T(8,128)S(1)}, u32[]{:S(2)}, u32[]{:S(2)}) collective-permute-start(f32[2,1,32,128]{3,2,1,0:T(8,128)S(1)} %shard_map.68), channel_id=1, source_target_pairs={{0,16},{16,0},{1,17},{17,1},{2,18},{18,2},{3,19},{19,3},{4,20},{20... | collective-permute-start | bytes 98312 | tf_op jit(solution)/shard_map/ppermute | solution.py:304
  41.0 2.0 %make_own.1 = (bf16[128,5632]{1,0:T(8,128)(2,1)S(1)}, bf16[32,5632]{1,0:T(8,128)(2,1)S(1)}, bf16[32,5632]{1,0:T(8,128)(2,1)S(1)}, f32[2,4,6,128]{3,2,1,0:T(8,128)S(1)}) custom-call(s32[12]{0:T(128)} %query_hbm.3, s32[2,4,12]{2,1,0:T(4,128)} %pairs_hbm.3, bf16[1,128,7168]{2,1,0:T(8,128)(2,1)} %act.3, bf16[1,128,4096]{2,1,0:T(8,128)(2,1)} %grad.3, ...), custom_call_target="tpu_custom_call" | custom-call | tf_op jit(solution)/shard_map/make_own/pallas_call | solution.py:174
  43.1 1.0 %shard_map.64.refs_0_ = f32[2,1,32,128]{3,2,1,0:T(8,128)S(1)} custom-call(bf16[32,5632]{1,0:T(8,128)(2,1)S(1)} %get-tuple-element.16.refs_0_, bf16[32,5632]{1,0:T(8,128)(2,1)S(1)} %get-tuple-element.17.refs_1_, bf16[128,5632]{1,0:T(8,128)(2,1)S(1)} %get-tuple-element.18.refs_2_.refs_1_, bf16[128,5632]{1,0:T(8,128)(2,1)S(1)} %get-tuple-element.19.refs_3_), custom_call_target="tpu_custom_call" | custom-call | flops 92274688 | bytes 3604480 | tf_op jit(solution)/shard_map/pallas_call | solution.py:190
  44.1 0.6 %shard_map.67.refs_3_ = f32[2,1,32,128]{3,2,1,0:T(8,128)S(1)} custom-call(bf16[32,5632]{1,0:T(8,128)(2,1)S(1)} %collective-permute-done.4.refs_0_, bf16[128,5632]{1,0:T(8,128)(2,1)S(1)} %get-tuple-element.18.refs_2_.refs_1_), custom_call_target="tpu_custom_call" | custom-call | flops 46137344 | bytes 1802240 | tf_op jit(solution)/shard_map/pallas_call | solution.py:190
  44.7 0.6 %shard_map.65.refs_1_ = f32[2,2,32,128]{3,2,1,0:T(8,128)S(1)} custom-call(bf16[32,5632]{1,0:T(8,128)(2,1)S(1)} %collective-permute-done.refs_0_, bf16[32,5632]{1,0:T(8,128)(2,1)S(1)} %collective-permute-done.1.refs_1_, bf16[128,5632]{1,0:T(8,128)(2,1)S(1)} %get-tuple-element.18.refs_2_.refs_1_), custom_call_target="tpu_custom_call" | custom-call | flops 92274688 | bytes 2162688 | tf_op jit(solution)/shard_map/pallas_call | solution.py:190
  45.3 0.0 collective-permute-done.5.refs_4_
  45.3 0.0 collective-permute-done.3.refs_2_
  45.3 0.1 collective-permute-start.6
  45.4 1.3 %collective-permute-done.6.refs_1_ = f32[2,4,32,128]{3,2,1,0:T(8,128)S(1)} collective-permute-done((f32[2,4,32,128]{3,2,1,0:T(8,128)S(1)}, f32[2,4,32,128]{3,2,1,0:T(8,128)S(1)}, u32[]{:S(2)}, u32[]{:S(2)}) %collective-permute-start.6) | collective-permute-done | bytes 131104 | tf_op jit(solution)/shard_map/ppermute | solution.py:312
  46.8 1.6 %collective-permute-start.7 = (f32[6,128]{1,0:T(8,128)S(1)}, f32[6,128]{1,0:T(8,128)S(1)}, u32[]{:S(2)}, u32[]{:S(2)}) collective-permute-start(f32[6,128]{1,0:T(8,128)S(1)} %get-tuple-element.24), channel_id=1, source_target_pairs={{0,2},{2,0},{1,3},{3,1},{4,6},{6,4},{5,7},{7,5},{8,10},{10,8},{9,1... | collective-permute-start | bytes 9224 | tf_op jit(solution)/shard_map/ppermute | solution.py:317
  48.3 2.1 %collective-permute-done.7 = f32[6,128]{1,0:T(8,128)S(1)} collective-permute-done((f32[6,128]{1,0:T(8,128)S(1)}, f32[6,128]{1,0:T(8,128)S(1)}, u32[]{:S(2)}, u32[]{:S(2)}) %collective-permute-start.7) | collective-permute-done | bytes 3104 | tf_op jit(solution)/shard_map/ppermute | solution.py:317
  50.5 0.6 %add_bitcast_fusion = f32[128,6]{0,1:T(8,128)} fusion(f32[6,128]{1,0:T(8,128)S(1)} %get-tuple-element.23, f32[6,128]{1,0:T(8,128)S(1)} %collective-permute-done.7), kind=kLoop, calls=%fused_computation | loop fusion | flops 768 | bytes 9216 | tf_op jit(solution)/shard_map/transpose | solution.py:318
  (2 shorter events, 0.1 us)
Async XLA Ops:
  1.7 34.6 %collective-permute-start.2 = (bf16[128,5632]{1,0:T(8,128)(2,1)S(1)}, bf16[128,5632]{1,0:T(8,128)(2,1)S(1)}, u32[]{:S(2)}, u32[]{:S(2)}) collective-permute-start(bf16[128,5632]{1,0:T(8,128)(2,1)S(1)} %get-tuple-element.19.refs_3_), channel_id=1, source_target_pairs={{0,16},{16,0},{1,17},{17,1},{2,18},{18,2},{3,19},{19,3},{4,20},{20... | collective-permute-start | bytes 4325384 | tf_op jit(solution)/shard_map/ppermute | solution.py:289
  4.8 10.4 %collective-permute-start = (bf16[32,5632]{1,0:T(8,128)(2,1)S(1)}, bf16[32,5632]{1,0:T(8,128)(2,1)S(1)}, u32[]{:S(2)}, u32[]{:S(2)}) collective-permute-start(bf16[32,5632]{1,0:T(8,128)(2,1)S(1)} %get-tuple-element.20), channel_id=1, source_target_pairs={{0,4},{4,0},{8,12},{12,8},{1,5},{5,1},{9,13},{13,9},{2,6},{6,2},{1... | collective-permute-start | bytes 1081352 | tf_op jit(solution)/shard_map/ppermute | solution.py:293
  6.4 19.6 %collective-permute-start.1 = (bf16[32,5632]{1,0:T(8,128)(2,1)S(1)}, bf16[32,5632]{1,0:T(8,128)(2,1)S(1)}, u32[]{:S(2)}, u32[]{:S(2)}) collective-permute-start(bf16[32,5632]{1,0:T(8,128)(2,1)S(1)} %get-tuple-element.21), channel_id=1, source_target_pairs={{0,12},{4,8},{8,4},{12,0},{1,13},{5,9},{9,5},{13,1},{2,14},{6,10},... | collective-permute-start | bytes 1081352 | tf_op jit(solution)/shard_map/ppermute | solution.py:293
  8.8 31.1 %collective-permute-start.4 = (bf16[32,5632]{1,0:T(8,128)(2,1)S(1)}, bf16[32,5632]{1,0:T(8,128)(2,1)S(1)}, u32[]{:S(2)}, u32[]{:S(2)}) collective-permute-start(bf16[32,5632]{1,0:T(8,128)(2,1)S(1)} %get-tuple-element.22), channel_id=1, source_target_pairs={{0,8},{4,12},{8,0},{12,4},{1,9},{5,13},{9,1},{13,5},{2,10},{6,14},... | collective-permute-start | bytes 1081352 | tf_op jit(solution)/shard_map/ppermute | solution.py:293
  37.0 8.3 %collective-permute-start.3 = (f32[2,2,32,128]{3,2,1,0:T(8,128)S(1)}, f32[2,2,32,128]{3,2,1,0:T(8,128)S(1)}, u32[]{:S(2)}, u32[]{:S(2)}) collective-permute-start(f32[2,2,32,128]{3,2,1,0:T(8,128)S(1)} %shard_map.66), channel_id=1, source_target_pairs={{0,16},{16,0},{1,17},{17,1},{2,18},{18,2},{3,19},{19,3},{4,20},{20... | collective-permute-start | bytes 196616 | tf_op jit(solution)/shard_map/ppermute | solution.py:304
  40.5 4.8 %collective-permute-start.5 = (f32[2,1,32,128]{3,2,1,0:T(8,128)S(1)}, f32[2,1,32,128]{3,2,1,0:T(8,128)S(1)}, u32[]{:S(2)}, u32[]{:S(2)}) collective-permute-start(f32[2,1,32,128]{3,2,1,0:T(8,128)S(1)} %shard_map.68), channel_id=1, source_target_pairs={{0,16},{16,0},{1,17},{17,1},{2,18},{18,2},{3,19},{19,3},{4,20},{20... | collective-permute-start | bytes 98312 | tf_op jit(solution)/shard_map/ppermute | solution.py:304
  45.3 1.4 %collective-permute-start.6 = (f32[2,4,32,128]{3,2,1,0:T(8,128)S(1)}, f32[2,4,32,128]{3,2,1,0:T(8,128)S(1)}, u32[]{:S(2)}, u32[]{:S(2)}) collective-permute-start(f32[2,4,32,128]{3,2,1,0:T(8,128)S(1)} %shard_map.69.refs_0_), channel_id=1, source_target_pairs={{0,1},{1,0},{2,3},{3,2},{4,5},{5,4},{6,7},{7,6},{8,9},{9,8},{10,11... | collective-permute-start | bytes 393224 | tf_op jit(solution)/shard_map/ppermute | solution.py:312
  46.8 3.7 %collective-permute-start.7 = (f32[6,128]{1,0:T(8,128)S(1)}, f32[6,128]{1,0:T(8,128)S(1)}, u32[]{:S(2)}, u32[]{:S(2)}) collective-permute-start(f32[6,128]{1,0:T(8,128)S(1)} %get-tuple-element.24), channel_id=1, source_target_pairs={{0,2},{2,0},{1,3},{3,1},{4,6},{6,4},{5,7},{7,5},{8,10},{10,8},{9,1... | collective-permute-start | bytes 9224 | tf_op jit(solution)/shard_map/ppermute | solution.py:317

commit v3 on v2

--- a/solution.py
+++ b/solution.py
@@ -252,13 +252,24 @@
     return vmem_call(kernel, [shape], [piece for group in groups for piece in group])[0]
 
 
-def score_kernel(weights, *refs):
+def score_kernel(whole_count, weights, *refs):
     layers, slots = weights.shape[:2]
     pieces, outs = refs[:-layers], refs[-layers:]
-    total = pieces[0][...]
-    for piece in pieces[1:]:
-        total = total + piece[...]
-    scores = [jnp.sum(total[0, k] * total[1, k], axis=0, keepdims=True) for k in range(slots)]
+
+    def add(refs):
+        total = refs[0][...]
+        for ref in refs[1:]:
+            total = total + ref[...]
+        return total
+
+    total, parted = add(pieces[:whole_count]), pieces[whole_count:]
+    scores = []
+    if parted:
+        last = add(parted)
+        first = slots - last.shape[1]
+        last = total[:, first:] + last
+        scores = [jnp.sum(last[0, k] * last[1, k], axis=0, keepdims=True) for k in range(slots - first)]
+    scores = [jnp.sum(total[0, k] * total[1, k], axis=0, keepdims=True) for k in range(slots - len(scores))] + scores
     for e, out in enumerate(outs):
         block = weights[e, 0] * scores[0]
         for k in range(1, slots):
@@ -266,9 +277,10 @@
         out[...] = block
 
 
-def make_scores(weights, pieces):
+def make_scores(weights, whole, parted):
     layers, _, wide, tokens = weights.shape
-    return vmem_call(score_kernel, [(wide, tokens)] * layers, [weights, *pieces])
+    kernel = functools.partial(score_kernel, len(whole))
+    return vmem_call(kernel, [(wide, tokens)] * layers, [weights, *whole, *parted])
 
 
 def shards(act_in, grad_out, factor_in, factor_out, query_row, pairs):
@@ -294,23 +306,19 @@
     own_rows, *own_slots, weights = make_own(early + late, *args)
 
     groups = [[project_local(own_slots, [own_rows] + list(sent_rows), wide_out)]]
-
-    def sums(numbers):
-        if not numbers:
-            return
-        group = []
-        for e, block in enumerate(rows, 1):
-            part_sums = project([slots[j] for j in numbers], block, wide_out)
-            group.append(lax.ppermute(part_sums, "parts", shifted((parts,), (parts - e,))))
-        group.insert(0, project([slots[j] for j in numbers], own_rows, wide_out))
-        groups.append(group)
-
-    sums(early[1:])
-    sums(late)
-    whole = [join(groups)]
+    early_group, late_group, late_got = [], [], []
+    for e, block in enumerate(rows, 1):
+        part_sums = project([slots[j] for j in early[1:]], block, wide_out)
+        early_group.append(lax.ppermute(part_sums, "parts", shifted((parts,), (parts - e,))))
+        part_sums = project([slots[j] for j in late], block, wide_out)
+        for f in range(subs):
+            late_got.append(lax.ppermute(part_sums, ("parts", "sub"), shifted((parts, subs), (parts - e, f))))
+    early_group.insert(0, project([slots[j] for j in early[1:]], own_rows, wide_out))
+    late_group.append(project([slots[j] for j in late], own_rows, wide_out))
+    whole = [join([*groups, early_group, late_group])]
     for f in range(1, subs):
         whole.append(lax.ppermute(whole[0], "sub", shifted((subs,), (f,))))
-    blocks = make_scores(weights, whole)
+    blocks = make_scores(weights, whole, late_got)
 
     out = blocks[0]
     for e in range(1, layers):

time: 51.2 us -> 52.6 us (1.027)
  starting transfers between devices: 11.2 us -> 12.9 us
    ppermute x2 -> x3, waiting for transfers between devices: 0.01 us -> 2.27 us  [the longest x2 2.27 us: shards(): lax.ppermute(part_sums, ('parts', 'sub'), shifted((parts, subs), (parts -...]
    ppermute x2 -> x3, starting transfers between devices: 2.33 us -> 3.95 us  [the longest x2 2.15 us: shards(): lax.ppermute(part_sums, ('parts', 'sub'), shifted((parts, subs), (parts -...]
    ppermute x1, waiting for transfers between devices: 1.33 us -> 0.01 us  [shards(): whole.append(lax.ppermute(whole[0], 'sub', shifted((subs,), (f,))))]
    ppermute x3, waiting for transfers between devices: 18.2 us -> 17 us  [shards(): slots[j] = lax.ppermute(sent_slots[j - 1], 'shard', to)]
  transfers between devices with their start and end apart: 8 -> 9, of which waited for: 6 -> 6; matrix products, arithmetic and copies ran while one was open for 0% -> 0% of each run, Pallas kernels for 10% -> 10%
where the time goes in v3:
time: 52.6 us; the launch traced here: 52.4 us
  waiting for transfers between devices  31.7 us (60%)
  starting transfers between devices  12.9 us (25%)
  Pallas kernels  7.11 us (14%)
  other arithmetic  0.6 us (1%)
    ppermute x3, waiting for transfers between devices, shards(): slots[j] = lax.ppermute(sent_slots[j - 1], 'shard', to)  17 us
    ppermute x1, waiting for transfers between devices, shards(): lax.ppermute(sent_rows[e - 1], 'parts', shifted((parts,), (e,)))  10.5 us
    ppermute x3, starting transfers between devices, shards(): slots[j] = lax.ppermute(sent_slots[j - 1], 'shard', to)  4.17 us
    pallas_call x7, Pallas kernels, vmem_call(): pl.pallas_call(kernel, out_shape=[pltpu.VMEM(shape, jnp.float32) for shap...  3.36 us
    ppermute x1, starting transfers between devices, shards(): lax.ppermute(sent_rows[e - 1], 'parts', shifted((parts,), (e,)))  3.06 us
    ppermute x2, waiting for transfers between devices, shards(): lax.ppermute(part_sums, ('parts', 'sub'), shifted((parts, subs), (parts -...  2.27 us
    ppermute x2, starting transfers between devices, shards(): lax.ppermute(part_sums, ('parts', 'sub'), shifted((parts, subs), (parts -...  2.15 us
    pallas_call x1, Pallas kernels, make_own(): pl.pallas_call(functools.partial(own_kernel, parts, tuple(order)), out_sh...  2.03 us
  transfers between devices with their start and end apart: 9, of which 6 were waited for; matrix products, arithmetic and copies ran while one was open for 0% of the time, Pallas kernels for 10%

profile of v3, /device:TPU:0, one launch (start us, length us, event | category | flops | bytes accessed | tf_op | source)
XLA Modules:
  0.0 52.4 jit_solution(1940592651761011297)
XLA Ops:
  0.0 1.7 %make_sends.1 = (bf16[32,5632]{1,0:T(8,128)(2,1)S(1)}, bf16[32,5632]{1,0:T(8,128)(2,1)S(1)}, bf16[32,5632]{1,0:T(8,128)(2,1)S(1)}, bf16[128,5632]{1,0:T(8,128)(2,1)S(1)}) custom-call(s32[12]{0:T(128)} %query_hbm.3, s32[2,4,12]{2,1,0:T(4,128)} %pairs_hbm.3, bf16[1,128,7168]{2,1,0:T(8,128)(2,1)} %act.3, bf16[1,128,4096]{2,1,0:T(8,128)(2,1)} %grad.3, ...), custom_call_target="tpu_custom_call" | custom-call | tf_op jit(solution)/shard_map/make_sends/pallas_call | solution.py:110
  1.7 3.1 %collective-permute-start.2 = (bf16[128,5632]{1,0:T(8,128)(2,1)S(1)}, bf16[128,5632]{1,0:T(8,128)(2,1)S(1)}, u32[]{:S(2)}, u32[]{:S(2)}) collective-permute-start(bf16[128,5632]{1,0:T(8,128)(2,1)S(1)} %get-tuple-element.19.refs_3_), channel_id=1, source_target_pairs={{0,16},{16,0},{1,17},{17,1},{2,18},{18,2},{3,19},{19,3},{4,20},{20... | collective-permute-start | bytes 4325384 | tf_op jit(solution)/shard_map/ppermute | solution.py:301
  4.8 1.6 %collective-permute-start = (bf16[32,5632]{1,0:T(8,128)(2,1)S(1)}, bf16[32,5632]{1,0:T(8,128)(2,1)S(1)}, u32[]{:S(2)}, u32[]{:S(2)}) collective-permute-start(bf16[32,5632]{1,0:T(8,128)(2,1)S(1)} %get-tuple-element.20), channel_id=1, source_target_pairs={{0,4},{4,0},{8,12},{12,8},{1,5},{5,1},{9,13},{13,9},{2,6},{6,2},{1... | collective-permute-start | bytes 1081352 | tf_op jit(solution)/shard_map/ppermute | solution.py:305
  6.4 2.5 %collective-permute-start.1 = (bf16[32,5632]{1,0:T(8,128)(2,1)S(1)}, bf16[32,5632]{1,0:T(8,128)(2,1)S(1)}, u32[]{:S(2)}, u32[]{:S(2)}) collective-permute-start(bf16[32,5632]{1,0:T(8,128)(2,1)S(1)} %get-tuple-element.21), channel_id=1, source_target_pairs={{0,12},{4,8},{8,4},{12,0},{1,13},{5,9},{9,5},{13,1},{2,14},{6,10},... | collective-permute-start | bytes 1081352 | tf_op jit(solution)/shard_map/ppermute | solution.py:305
  8.8 0.1 collective-permute-start.4
  9.0 6.2 %collective-permute-done.refs_0_ = bf16[32,5632]{1,0:T(8,128)(2,1)S(1)} collective-permute-done((bf16[32,5632]{1,0:T(8,128)(2,1)S(1)}, bf16[32,5632]{1,0:T(8,128)(2,1)S(1)}, u32[]{:S(2)}, u32[]{:S(2)}) %collective-permute-start) | collective-permute-done | bytes 360480 | tf_op jit(solution)/shard_map/ppermute | solution.py:305
  15.2 10.8 %collective-permute-done.1.refs_1_ = bf16[32,5632]{1,0:T(8,128)(2,1)S(1)} collective-permute-done((bf16[32,5632]{1,0:T(8,128)(2,1)S(1)}, bf16[32,5632]{1,0:T(8,128)(2,1)S(1)}, u32[]{:S(2)}, u32[]{:S(2)}) %collective-permute-start.1) | collective-permute-done | bytes 360480 | tf_op jit(solution)/shard_map/ppermute | solution.py:305
  25.9 10.5 %collective-permute-done.2.refs_2_.refs_1_ = bf16[128,5632]{1,0:T(8,128)(2,1)S(1)} collective-permute-done((bf16[128,5632]{1,0:T(8,128)(2,1)S(1)}, bf16[128,5632]{1,0:T(8,128)(2,1)S(1)}, u32[]{:S(2)}, u32[]{:S(2)}) %collective-permute-start.2) | collective-permute-done | bytes 1441824 | tf_op jit(solution)/shard_map/ppermute | solution.py:301
  36.4 0.6 %shard_map.66 = f32[2,2,32,128]{3,2,1,0:T(8,128)S(1)} custom-call(bf16[32,5632]{1,0:T(8,128)(2,1)S(1)} %collective-permute-done.refs_0_, bf16[32,5632]{1,0:T(8,128)(2,1)S(1)} %collective-permute-done.1.refs_1_, bf16[128,5632]{1,0:T(8,128)(2,1)S(1)} %collective-permute-done.2.refs_2_.refs_1_), custom_call_target="tpu_custom_call" | custom-call | flops 92274688 | bytes 2162688 | tf_op jit(solution)/shard_map/pallas_call | solution.py:190
  37.0 1.8 %collective-permute-start.3 = (f32[2,2,32,128]{3,2,1,0:T(8,128)S(1)}, f32[2,2,32,128]{3,2,1,0:T(8,128)S(1)}, u32[]{:S(2)}, u32[]{:S(2)}) collective-permute-start(f32[2,2,32,128]{3,2,1,0:T(8,128)S(1)} %shard_map.66), channel_id=1, source_target_pairs={{0,16},{16,0},{1,17},{17,1},{2,18},{18,2},{3,19},{19,3},{4,20},{20... | collective-permute-start | bytes 196616 | tf_op jit(solution)/shard_map/ppermute | solution.py:312
  38.8 2.0 %make_own.1 = (bf16[128,5632]{1,0:T(8,128)(2,1)S(1)}, bf16[32,5632]{1,0:T(8,128)(2,1)S(1)}, bf16[32,5632]{1,0:T(8,128)(2,1)S(1)}, f32[2,4,6,128]{3,2,1,0:T(8,128)S(1)}) custom-call(s32[12]{0:T(128)} %query_hbm.3, s32[2,4,12]{2,1,0:T(4,128)} %pairs_hbm.3, bf16[1,128,7168]{2,1,0:T(8,128)(2,1)} %act.3, bf16[1,128,4096]{2,1,0:T(8,128)(2,1)} %grad.3, ...), custom_call_target="tpu_custom_call" | custom-call | tf_op jit(solution)/shard_map/make_own/pallas_call | solution.py:174
  40.8 1.0 %shard_map.64.refs_0_ = f32[2,1,32,128]{3,2,1,0:T(8,128)S(1)} custom-call(bf16[32,5632]{1,0:T(8,128)(2,1)S(1)} %get-tuple-element.16.refs_0_, bf16[32,5632]{1,0:T(8,128)(2,1)S(1)} %get-tuple-element.17.refs_1_, bf16[128,5632]{1,0:T(8,128)(2,1)S(1)} %get-tuple-element.18.refs_2_.refs_1_, bf16[128,5632]{1,0:T(8,128)(2,1)S(1)} %get-tuple-element.19.refs_3_), custom_call_target="tpu_custom_call" | custom-call | flops 92274688 | bytes 3604480 | tf_op jit(solution)/shard_map/pallas_call | solution.py:190
  41.8 0.0 collective-permute-done.4.refs_0_
  41.9 0.5 %shard_map.67.refs_3_ = f32[2,1,32,128]{3,2,1,0:T(8,128)S(1)} custom-call(bf16[32,5632]{1,0:T(8,128)(2,1)S(1)} %collective-permute-done.4.refs_0_, bf16[128,5632]{1,0:T(8,128)(2,1)S(1)} %get-tuple-element.18.refs_2_.refs_1_), custom_call_target="tpu_custom_call" | custom-call | flops 46137344 | bytes 1802240 | tf_op jit(solution)/shard_map/pallas_call | solution.py:190
  42.4 0.6 %shard_map.65.refs_1_ = f32[2,2,32,128]{3,2,1,0:T(8,128)S(1)} custom-call(bf16[32,5632]{1,0:T(8,128)(2,1)S(1)} %collective-permute-done.refs_0_, bf16[32,5632]{1,0:T(8,128)(2,1)S(1)} %collective-permute-done.1.refs_1_, bf16[128,5632]{1,0:T(8,128)(2,1)S(1)} %get-tuple-element.18.refs_2_.refs_1_), custom_call_target="tpu_custom_call" | custom-call | flops 92274688 | bytes 2162688 | tf_op jit(solution)/shard_map/pallas_call | solution.py:190
  43.0 0.0 collective-permute-done.3.refs_2_
  43.1 0.1 collective-permute-start.5
  43.1 0.5 %shard_map.69 = f32[2,1,32,128]{3,2,1,0:T(8,128)S(1)} custom-call(bf16[32,5632]{1,0:T(8,128)(2,1)S(1)} %collective-permute-done.4.refs_0_, bf16[128,5632]{1,0:T(8,128)(2,1)S(1)} %collective-permute-done.2.refs_2_.refs_1_), custom_call_target="tpu_custom_call" | custom-call | flops 46137344 | bytes 1802240 | tf_op jit(solution)/shard_map/pallas_call | solution.py:190
  43.7 0.4 collective-permute-start.7
  44.1 1.7 %collective-permute-start.6 = (f32[2,1,32,128]{3,2,1,0:T(8,128)S(1)}, f32[2,1,32,128]{3,2,1,0:T(8,128)S(1)}, u32[]{:S(2)}, u32[]{:S(2)}) collective-permute-start(f32[2,1,32,128]{3,2,1,0:T(8,128)S(1)} %shard_map.69), channel_id=1, source_target_pairs={{0,16},{1,17},{16,0},{17,1},{2,18},{3,19},{18,2},{19,3},{4,20},{5,... | collective-permute-start | bytes 98312 | tf_op jit(solution)/shard_map/ppermute | solution.py:315
  45.8 1.2 %collective-permute-done.7.refs_3_ = f32[2,1,32,128]{3,2,1,0:T(8,128)S(1)} collective-permute-done((f32[2,1,32,128]{3,2,1,0:T(8,128)S(1)}, f32[2,1,32,128]{3,2,1,0:T(8,128)S(1)}, u32[]{:S(2)}, u32[]{:S(2)}) %collective-permute-start.7) | collective-permute-done | bytes 32800 | tf_op jit(solution)/shard_map/ppermute | solution.py:315
  47.0 1.1 %collective-permute-done.6.refs_2_ = f32[2,1,32,128]{3,2,1,0:T(8,128)S(1)} collective-permute-done((f32[2,1,32,128]{3,2,1,0:T(8,128)S(1)}, f32[2,1,32,128]{3,2,1,0:T(8,128)S(1)}, u32[]{:S(2)}, u32[]{:S(2)}) %collective-permute-start.6) | collective-permute-done | bytes 32800 | tf_op jit(solution)/shard_map/ppermute | solution.py:315
  48.1 0.0 collective-permute-done.5.refs_1_
  48.1 1.7 %collective-permute-start.8 = (f32[6,128]{1,0:T(8,128)S(1)}, f32[6,128]{1,0:T(8,128)S(1)}, u32[]{:S(2)}, u32[]{:S(2)}) collective-permute-start(f32[6,128]{1,0:T(8,128)S(1)} %get-tuple-element.24), channel_id=1, source_target_pairs={{0,2},{2,0},{1,3},{3,1},{4,6},{6,4},{5,7},{7,5},{8,10},{10,8},{9,1... | collective-permute-start | bytes 9224 | tf_op jit(solution)/shard_map/ppermute | solution.py:325
  49.8 2.0 %collective-permute-done.8 = f32[6,128]{1,0:T(8,128)S(1)} collective-permute-done((f32[6,128]{1,0:T(8,128)S(1)}, f32[6,128]{1,0:T(8,128)S(1)}, u32[]{:S(2)}, u32[]{:S(2)}) %collective-permute-start.8) | collective-permute-done | bytes 3104 | tf_op jit(solution)/shard_map/ppermute | solution.py:325
  51.8 0.6 %add_bitcast_fusion = f32[128,6]{0,1:T(8,128)} fusion(f32[6,128]{1,0:T(8,128)S(1)} %get-tuple-element.23, f32[6,128]{1,0:T(8,128)S(1)} %collective-permute-done.8), kind=kLoop, calls=%fused_computation | loop fusion | flops 768 | bytes 9216 | tf_op jit(solution)/shard_map/transpose | solution.py:326
  (2 shorter events, 0.1 us)
Async XLA Ops:
  1.7 34.6 %collective-permute-start.2 = (bf16[128,5632]{1,0:T(8,128)(2,1)S(1)}, bf16[128,5632]{1,0:T(8,128)(2,1)S(1)}, u32[]{:S(2)}, u32[]{:S(2)}) collective-permute-start(bf16[128,5632]{1,0:T(8,128)(2,1)S(1)} %get-tuple-element.19.refs_3_), channel_id=1, source_target_pairs={{0,16},{16,0},{1,17},{17,1},{2,18},{18,2},{3,19},{19,3},{4,20},{20... | collective-permute-start | bytes 4325384 | tf_op jit(solution)/shard_map/ppermute | solution.py:301
  4.8 10.4 %collective-permute-start = (bf16[32,5632]{1,0:T(8,128)(2,1)S(1)}, bf16[32,5632]{1,0:T(8,128)(2,1)S(1)}, u32[]{:S(2)}, u32[]{:S(2)}) collective-permute-start(bf16[32,5632]{1,0:T(8,128)(2,1)S(1)} %get-tuple-element.20), channel_id=1, source_target_pairs={{0,4},{4,0},{8,12},{12,8},{1,5},{5,1},{9,13},{13,9},{2,6},{6,2},{1... | collective-permute-start | bytes 1081352 | tf_op jit(solution)/shard_map/ppermute | solution.py:305
  6.4 19.6 %collective-permute-start.1 = (bf16[32,5632]{1,0:T(8,128)(2,1)S(1)}, bf16[32,5632]{1,0:T(8,128)(2,1)S(1)}, u32[]{:S(2)}, u32[]{:S(2)}) collective-permute-start(bf16[32,5632]{1,0:T(8,128)(2,1)S(1)} %get-tuple-element.21), channel_id=1, source_target_pairs={{0,12},{4,8},{8,4},{12,0},{1,13},{5,9},{9,5},{13,1},{2,14},{6,10},... | collective-permute-start | bytes 1081352 | tf_op jit(solution)/shard_map/ppermute | solution.py:305
  8.8 33.0 %collective-permute-start.4 = (bf16[32,5632]{1,0:T(8,128)(2,1)S(1)}, bf16[32,5632]{1,0:T(8,128)(2,1)S(1)}, u32[]{:S(2)}, u32[]{:S(2)}) collective-permute-start(bf16[32,5632]{1,0:T(8,128)(2,1)S(1)} %get-tuple-element.22), channel_id=1, source_target_pairs={{0,8},{4,12},{8,0},{12,4},{1,9},{5,13},{9,1},{13,5},{2,10},{6,14},... | collective-permute-start | bytes 1081352 | tf_op jit(solution)/shard_map/ppermute | solution.py:305
  37.0 6.1 %collective-permute-start.3 = (f32[2,2,32,128]{3,2,1,0:T(8,128)S(1)}, f32[2,2,32,128]{3,2,1,0:T(8,128)S(1)}, u32[]{:S(2)}, u32[]{:S(2)}) collective-permute-start(f32[2,2,32,128]{3,2,1,0:T(8,128)S(1)} %shard_map.66), channel_id=1, source_target_pairs={{0,16},{16,0},{1,17},{17,1},{2,18},{18,2},{3,19},{19,3},{4,20},{20... | collective-permute-start | bytes 196616 | tf_op jit(solution)/shard_map/ppermute | solution.py:312
  43.1 5.0 %collective-permute-start.5 = (f32[2,4,32,128]{3,2,1,0:T(8,128)S(1)}, f32[2,4,32,128]{3,2,1,0:T(8,128)S(1)}, u32[]{:S(2)}, u32[]{:S(2)}) collective-permute-start(f32[2,4,32,128]{3,2,1,0:T(8,128)S(1)} %shard_map.68.refs_0_), channel_id=1, source_target_pairs={{0,1},{1,0},{2,3},{3,2},{4,5},{5,4},{6,7},{7,6},{8,9},{9,8},{10,11... | collective-permute-start | bytes 393224 | tf_op jit(solution)/shard_map/ppermute | solution.py:320
  43.7 3.4 %collective-permute-start.7 = (f32[2,1,32,128]{3,2,1,0:T(8,128)S(1)}, f32[2,1,32,128]{3,2,1,0:T(8,128)S(1)}, u32[]{:S(2)}, u32[]{:S(2)}) collective-permute-start(f32[2,1,32,128]{3,2,1,0:T(8,128)S(1)} %shard_map.69), channel_id=1, source_target_pairs={{0,17},{1,16},{16,1},{17,0},{2,19},{3,18},{18,3},{19,2},{4,21},{5,... | collective-permute-start | bytes 98312 | tf_op jit(solution)/shard_map/ppermute | solution.py:315
  44.1 4.0 %collective-permute-start.6 = (f32[2,1,32,128]{3,2,1,0:T(8,128)S(1)}, f32[2,1,32,128]{3,2,1,0:T(8,128)S(1)}, u32[]{:S(2)}, u32[]{:S(2)}) collective-permute-start(f32[2,1,32,128]{3,2,1,0:T(8,128)S(1)} %shard_map.69), channel_id=1, source_target_pairs={{0,16},{1,17},{16,0},{17,1},{2,18},{3,19},{18,2},{19,3},{4,20},{5,... | collective-permute-start | bytes 98312 | tf_op jit(solution)/shard_map/ppermute | solution.py:315
  48.1 3.7 %collective-permute-start.8 = (f32[6,128]{1,0:T(8,128)S(1)}, f32[6,128]{1,0:T(8,128)S(1)}, u32[]{:S(2)}, u32[]{:S(2)}) collective-permute-start(f32[6,128]{1,0:T(8,128)S(1)} %get-tuple-element.24), channel_id=1, source_target_pairs={{0,2},{2,0},{1,3},{3,1},{4,6},{6,4},{5,7},{7,5},{8,10},{10,8},{9,1... | collective-permute-start | bytes 9224 | tf_op jit(solution)/shard_map/ppermute | solution.py:325

commit v4 on v3

--- a/solution.py
+++ b/solution.py
@@ -33,12 +33,12 @@
 
 
 def slot_groups(n):
-    late = [n // 2] if n > 1 else []
+    late = [n - 1] if n > 1 else []
     return [j for j in range(n) if j not in late], late
 
 
 def start_order(n):
-    return list(range(n - 1, n // 2 - 1, -1)) + list(range(1, n // 2))
+    return list(range(max(1, n // 2), n)) + list(range(1, n // 2))
 
 
 def start_tables(query_hbm, pairs_hbm, query_row, pairs, sem):
@@ -309,7 +309,8 @@
     early_group, late_group, late_got = [], [], []
     for e, block in enumerate(rows, 1):
         part_sums = project([slots[j] for j in early[1:]], block, wide_out)
-        early_group.append(lax.ppermute(part_sums, "parts", shifted((parts,), (parts - e,))))
+        to = shifted((parts, subs), (parts - e, 1 % subs))
+        early_group.append(lax.ppermute(part_sums, ("parts", "sub"), to))
         part_sums = project([slots[j] for j in late], block, wide_out)
         for f in range(subs):
             late_got.append(lax.ppermute(part_sums, ("parts", "sub"), shifted((parts, subs), (parts - e, f))))

time: 52.6 us -> 52.7 us (level)
    ppermute x1, waiting for transfers between devices: 10.5 us -> 2.37 us  [shards(): lax.ppermute(sent_rows[e - 1], 'parts', shifted((parts,), (e,)))]
    ppermute x3, waiting for transfers between devices: 17 us -> 24.8 us  [shards(): slots[j] = lax.ppermute(sent_slots[j - 1], 'shard', to)]
    ppermute x1, starting transfers between devices: 0.07 us -> 1.59 us  [shards(): whole.append(lax.ppermute(whole[0], 'sub', shifted((subs,), (f,))))]
    ppermute x1, starting transfers between devices: 1.81 us -> 0.39 us  [shards(): early_group.append(lax.ppermute(part_sums, ('parts', 'sub'), to))]
where the time goes in v4:
time: 52.7 us; the launch traced here: 52.5 us
  waiting for transfers between devices  32.1 us (61%)
  starting transfers between devices  12.7 us (24%)
  Pallas kernels  7.11 us (13%)
  other arithmetic  0.6 us (1%)
    ppermute x3, waiting for transfers between devices, shards(): slots[j] = lax.ppermute(sent_slots[j - 1], 'shard', to)  24.8 us
    ppermute x3, starting transfers between devices, shards(): slots[j] = lax.ppermute(sent_slots[j - 1], 'shard', to)  4.39 us
    pallas_call x7, Pallas kernels, vmem_call(): pl.pallas_call(kernel, out_shape=[pltpu.VMEM(shape, jnp.float32) for shap...  3.36 us
    ppermute x1, starting transfers between devices, shards(): lax.ppermute(sent_rows[e - 1], 'parts', shifted((parts,), (e,)))  3.06 us
    ppermute x2, waiting for transfers between devices, shards(): lax.ppermute(part_sums, ('parts', 'sub'), shifted((parts, subs), (parts -...  2.75 us
    ppermute x1, waiting for transfers between devices, shards(): lax.ppermute(sent_rows[e - 1], 'parts', shifted((parts,), (e,)))  2.37 us
    ppermute x1, waiting for transfers between devices, shards(): out = out + lax.ppermute(blocks[e], 'layer', shifted((layers,), (e,)))  2.12 us
    pallas_call x1, Pallas kernels, make_own(): pl.pallas_call(functools.partial(own_kernel, parts, tuple(order)), out_sh...  2.03 us
  transfers between devices with their start and end apart: 9, of which 6 were waited for; matrix products, arithmetic and copies ran while one was open for 0% of the time, Pallas kernels for 10%

profile of v4, /device:TPU:0, one launch (start us, length us, event | category | flops | bytes accessed | tf_op | source)
XLA Modules:
  0.0 52.5 jit_solution(1363620476824036626)
XLA Ops:
  0.0 1.7 %make_sends.1 = (bf16[32,5632]{1,0:T(8,128)(2,1)S(1)}, bf16[32,5632]{1,0:T(8,128)(2,1)S(1)}, bf16[32,5632]{1,0:T(8,128)(2,1)S(1)}, bf16[128,5632]{1,0:T(8,128)(2,1)S(1)}) custom-call(s32[12]{0:T(128)} %query_hbm.3, s32[2,4,12]{2,1,0:T(4,128)} %pairs_hbm.3, bf16[1,128,7168]{2,1,0:T(8,128)(2,1)} %act.3, bf16[1,128,4096]{2,1,0:T(8,128)(2,1)} %grad.3, ...), custom_call_target="tpu_custom_call" | custom-call | tf_op jit(solution)/shard_map/make_sends/pallas_call | solution.py:110
  1.7 3.1 %collective-permute-start.2 = (bf16[128,5632]{1,0:T(8,128)(2,1)S(1)}, bf16[128,5632]{1,0:T(8,128)(2,1)S(1)}, u32[]{:S(2)}, u32[]{:S(2)}) collective-permute-start(bf16[128,5632]{1,0:T(8,128)(2,1)S(1)} %get-tuple-element.19.refs_3_), channel_id=1, source_target_pairs={{0,16},{16,0},{1,17},{17,1},{2,18},{18,2},{3,19},{19,3},{4,20},{20... | collective-permute-start | bytes 4325384 | tf_op jit(solution)/shard_map/ppermute | solution.py:301
  4.8 1.6 %collective-permute-start = (bf16[32,5632]{1,0:T(8,128)(2,1)S(1)}, bf16[32,5632]{1,0:T(8,128)(2,1)S(1)}, u32[]{:S(2)}, u32[]{:S(2)}) collective-permute-start(bf16[32,5632]{1,0:T(8,128)(2,1)S(1)} %get-tuple-element.20), channel_id=1, source_target_pairs={{0,4},{4,0},{8,12},{12,8},{1,5},{5,1},{9,13},{13,9},{2,6},{6,2},{1... | collective-permute-start | bytes 1081352 | tf_op jit(solution)/shard_map/ppermute | solution.py:305
  6.4 2.6 %collective-permute-start.1 = (bf16[32,5632]{1,0:T(8,128)(2,1)S(1)}, bf16[32,5632]{1,0:T(8,128)(2,1)S(1)}, u32[]{:S(2)}, u32[]{:S(2)}) collective-permute-start(bf16[32,5632]{1,0:T(8,128)(2,1)S(1)} %get-tuple-element.21), channel_id=1, source_target_pairs={{0,8},{4,12},{8,0},{12,4},{1,9},{5,13},{9,1},{13,5},{2,10},{6,14},... | collective-permute-start | bytes 1081352 | tf_op jit(solution)/shard_map/ppermute | solution.py:305
  9.0 0.2 collective-permute-start.4
  9.2 12.3 %collective-permute-done.refs_0_ = bf16[32,5632]{1,0:T(8,128)(2,1)S(1)} collective-permute-done((bf16[32,5632]{1,0:T(8,128)(2,1)S(1)}, bf16[32,5632]{1,0:T(8,128)(2,1)S(1)}, u32[]{:S(2)}, u32[]{:S(2)}) %collective-permute-start) | collective-permute-done | bytes 360480 | tf_op jit(solution)/shard_map/ppermute | solution.py:305
  21.5 12.5 %collective-permute-done.1.refs_1_ = bf16[32,5632]{1,0:T(8,128)(2,1)S(1)} collective-permute-done((bf16[32,5632]{1,0:T(8,128)(2,1)S(1)}, bf16[32,5632]{1,0:T(8,128)(2,1)S(1)}, u32[]{:S(2)}, u32[]{:S(2)}) %collective-permute-start.1) | collective-permute-done | bytes 360480 | tf_op jit(solution)/shard_map/ppermute | solution.py:305
  34.0 2.4 %collective-permute-done.2.refs_2_.refs_1_ = bf16[128,5632]{1,0:T(8,128)(2,1)S(1)} collective-permute-done((bf16[128,5632]{1,0:T(8,128)(2,1)S(1)}, bf16[128,5632]{1,0:T(8,128)(2,1)S(1)}, u32[]{:S(2)}, u32[]{:S(2)}) %collective-permute-start.2) | collective-permute-done | bytes 1441824 | tf_op jit(solution)/shard_map/ppermute | solution.py:301
  36.4 0.6 %shard_map.66 = f32[2,2,32,128]{3,2,1,0:T(8,128)S(1)} custom-call(bf16[32,5632]{1,0:T(8,128)(2,1)S(1)} %collective-permute-done.refs_0_, bf16[32,5632]{1,0:T(8,128)(2,1)S(1)} %collective-permute-done.1.refs_1_, bf16[128,5632]{1,0:T(8,128)(2,1)S(1)} %collective-permute-done.2.refs_2_.refs_1_), custom_call_target="tpu_custom_call" | custom-call | flops 92274688 | bytes 2162688 | tf_op jit(solution)/shard_map/pallas_call | solution.py:190
  37.0 0.4 collective-permute-start.3
  37.4 2.0 %make_own.1 = (bf16[128,5632]{1,0:T(8,128)(2,1)S(1)}, bf16[32,5632]{1,0:T(8,128)(2,1)S(1)}, bf16[32,5632]{1,0:T(8,128)(2,1)S(1)}, f32[2,4,6,128]{3,2,1,0:T(8,128)S(1)}) custom-call(s32[12]{0:T(128)} %query_hbm.3, s32[2,4,12]{2,1,0:T(4,128)} %pairs_hbm.3, bf16[1,128,7168]{2,1,0:T(8,128)(2,1)} %act.3, bf16[1,128,4096]{2,1,0:T(8,128)(2,1)} %grad.3, ...), custom_call_target="tpu_custom_call" | custom-call | tf_op jit(solution)/shard_map/make_own/pallas_call | solution.py:174
  39.4 1.0 %shard_map.64.refs_0_ = f32[2,1,32,128]{3,2,1,0:T(8,128)S(1)} custom-call(bf16[32,5632]{1,0:T(8,128)(2,1)S(1)} %get-tuple-element.16.refs_0_, bf16[32,5632]{1,0:T(8,128)(2,1)S(1)} %get-tuple-element.17.refs_1_, bf16[128,5632]{1,0:T(8,128)(2,1)S(1)} %get-tuple-element.18.refs_2_.refs_1_, bf16[128,5632]{1,0:T(8,128)(2,1)S(1)} %get-tuple-element.19.refs_3_), custom_call_target="tpu_custom_call" | custom-call | flops 92274688 | bytes 3604480 | tf_op jit(solution)/shard_map/pallas_call | solution.py:190
  40.4 0.0 collective-permute-done.4.refs_0_
  40.4 0.5 %shard_map.67.refs_3_ = f32[2,1,32,128]{3,2,1,0:T(8,128)S(1)} custom-call(bf16[32,5632]{1,0:T(8,128)(2,1)S(1)} %collective-permute-done.4.refs_0_, bf16[128,5632]{1,0:T(8,128)(2,1)S(1)} %get-tuple-element.18.refs_2_.refs_1_), custom_call_target="tpu_custom_call" | custom-call | flops 46137344 | bytes 1802240 | tf_op jit(solution)/shard_map/pallas_call | solution.py:190
  41.0 0.6 %shard_map.65.refs_1_ = f32[2,2,32,128]{3,2,1,0:T(8,128)S(1)} custom-call(bf16[32,5632]{1,0:T(8,128)(2,1)S(1)} %collective-permute-done.refs_0_, bf16[32,5632]{1,0:T(8,128)(2,1)S(1)} %collective-permute-done.1.refs_1_, bf16[128,5632]{1,0:T(8,128)(2,1)S(1)} %get-tuple-element.18.refs_2_.refs_1_), custom_call_target="tpu_custom_call" | custom-call | flops 92274688 | bytes 2162688 | tf_op jit(solution)/shard_map/pallas_call | solution.py:190
  41.6 0.0 collective-permute-done.3.refs_2_
  41.6 1.6 %collective-permute-start.5 = (f32[2,4,32,128]{3,2,1,0:T(8,128)S(1)}, f32[2,4,32,128]{3,2,1,0:T(8,128)S(1)}, u32[]{:S(2)}, u32[]{:S(2)}) collective-permute-start(f32[2,4,32,128]{3,2,1,0:T(8,128)S(1)} %shard_map.68.refs_0_), channel_id=1, source_target_pairs={{0,1},{1,0},{2,3},{3,2},{4,5},{5,4},{6,7},{7,6},{8,9},{9,8},{10,11... | collective-permute-start | bytes 393224 | tf_op jit(solution)/shard_map/ppermute | solution.py:321
  43.2 0.5 %shard_map.69 = f32[2,1,32,128]{3,2,1,0:T(8,128)S(1)} custom-call(bf16[32,5632]{1,0:T(8,128)(2,1)S(1)} %collective-permute-done.4.refs_0_, bf16[128,5632]{1,0:T(8,128)(2,1)S(1)} %collective-permute-done.2.refs_2_.refs_1_), custom_call_target="tpu_custom_call" | custom-call | flops 46137344 | bytes 1802240 | tf_op jit(solution)/shard_map/pallas_call | solution.py:190
  43.8 0.0 collective-permute-start.7
  43.8 1.6 %collective-permute-start.6 = (f32[2,1,32,128]{3,2,1,0:T(8,128)S(1)}, f32[2,1,32,128]{3,2,1,0:T(8,128)S(1)}, u32[]{:S(2)}, u32[]{:S(2)}) collective-permute-start(f32[2,1,32,128]{3,2,1,0:T(8,128)S(1)} %shard_map.69), channel_id=1, source_target_pairs={{0,16},{1,17},{16,0},{17,1},{2,18},{3,19},{18,2},{19,3},{4,20},{5,... | collective-permute-start | bytes 98312 | tf_op jit(solution)/shard_map/ppermute | solution.py:316
  45.4 1.8 %collective-permute-done.7.refs_3_ = f32[2,1,32,128]{3,2,1,0:T(8,128)S(1)} collective-permute-done((f32[2,1,32,128]{3,2,1,0:T(8,128)S(1)}, f32[2,1,32,128]{3,2,1,0:T(8,128)S(1)}, u32[]{:S(2)}, u32[]{:S(2)}) %collective-permute-start.7) | collective-permute-done | bytes 32800 | tf_op jit(solution)/shard_map/ppermute | solution.py:316
  47.3 0.9 %collective-permute-done.6.refs_2_ = f32[2,1,32,128]{3,2,1,0:T(8,128)S(1)} collective-permute-done((f32[2,1,32,128]{3,2,1,0:T(8,128)S(1)}, f32[2,1,32,128]{3,2,1,0:T(8,128)S(1)}, u32[]{:S(2)}, u32[]{:S(2)}) %collective-permute-start.6) | collective-permute-done | bytes 32800 | tf_op jit(solution)/shard_map/ppermute | solution.py:316
  48.2 0.0 collective-permute-done.5.refs_1_
  48.2 1.6 %collective-permute-start.8 = (f32[6,128]{1,0:T(8,128)S(1)}, f32[6,128]{1,0:T(8,128)S(1)}, u32[]{:S(2)}, u32[]{:S(2)}) collective-permute-start(f32[6,128]{1,0:T(8,128)S(1)} %get-tuple-element.24), channel_id=1, source_target_pairs={{0,2},{2,0},{1,3},{3,1},{4,6},{6,4},{5,7},{7,5},{8,10},{10,8},{9,1... | collective-permute-start | bytes 9224 | tf_op jit(solution)/shard_map/ppermute | solution.py:326
  49.8 2.1 %collective-permute-done.8 = f32[6,128]{1,0:T(8,128)S(1)} collective-permute-done((f32[6,128]{1,0:T(8,128)S(1)}, f32[6,128]{1,0:T(8,128)S(1)}, u32[]{:S(2)}, u32[]{:S(2)}) %collective-permute-start.8) | collective-permute-done | bytes 3104 | tf_op jit(solution)/shard_map/ppermute | solution.py:326
  51.9 0.6 %add_bitcast_fusion = f32[128,6]{0,1:T(8,128)} fusion(f32[6,128]{1,0:T(8,128)S(1)} %get-tuple-element.23, f32[6,128]{1,0:T(8,128)S(1)} %collective-permute-done.8), kind=kLoop, calls=%fused_computation | loop fusion | flops 768 | bytes 9216 | tf_op jit(solution)/shard_map/transpose | solution.py:327
  (2 shorter events, 0.1 us)
Async XLA Ops:
  1.7 34.6 %collective-permute-start.2 = (bf16[128,5632]{1,0:T(8,128)(2,1)S(1)}, bf16[128,5632]{1,0:T(8,128)(2,1)S(1)}, u32[]{:S(2)}, u32[]{:S(2)}) collective-permute-start(bf16[128,5632]{1,0:T(8,128)(2,1)S(1)} %get-tuple-element.19.refs_3_), channel_id=1, source_target_pairs={{0,16},{16,0},{1,17},{17,1},{2,18},{18,2},{3,19},{19,3},{4,20},{20... | collective-permute-start | bytes 4325384 | tf_op jit(solution)/shard_map/ppermute | solution.py:301
  4.8 16.7 %collective-permute-start = (bf16[32,5632]{1,0:T(8,128)(2,1)S(1)}, bf16[32,5632]{1,0:T(8,128)(2,1)S(1)}, u32[]{:S(2)}, u32[]{:S(2)}) collective-permute-start(bf16[32,5632]{1,0:T(8,128)(2,1)S(1)} %get-tuple-element.20), channel_id=1, source_target_pairs={{0,4},{4,0},{8,12},{12,8},{1,5},{5,1},{9,13},{13,9},{2,6},{6,2},{1... | collective-permute-start | bytes 1081352 | tf_op jit(solution)/shard_map/ppermute | solution.py:305
  6.4 27.6 %collective-permute-start.1 = (bf16[32,5632]{1,0:T(8,128)(2,1)S(1)}, bf16[32,5632]{1,0:T(8,128)(2,1)S(1)}, u32[]{:S(2)}, u32[]{:S(2)}) collective-permute-start(bf16[32,5632]{1,0:T(8,128)(2,1)S(1)} %get-tuple-element.21), channel_id=1, source_target_pairs={{0,8},{4,12},{8,0},{12,4},{1,9},{5,13},{9,1},{13,5},{2,10},{6,14},... | collective-permute-start | bytes 1081352 | tf_op jit(solution)/shard_map/ppermute | solution.py:305
  9.0 31.5 %collective-permute-start.4 = (bf16[32,5632]{1,0:T(8,128)(2,1)S(1)}, bf16[32,5632]{1,0:T(8,128)(2,1)S(1)}, u32[]{:S(2)}, u32[]{:S(2)}) collective-permute-start(bf16[32,5632]{1,0:T(8,128)(2,1)S(1)} %get-tuple-element.22), channel_id=1, source_target_pairs={{0,12},{4,8},{8,4},{12,0},{1,13},{5,9},{9,5},{13,1},{2,14},{6,10},... | collective-permute-start | bytes 1081352 | tf_op jit(solution)/shard_map/ppermute | solution.py:305
  37.0 4.6 %collective-permute-start.3 = (f32[2,2,32,128]{3,2,1,0:T(8,128)S(1)}, f32[2,2,32,128]{3,2,1,0:T(8,128)S(1)}, u32[]{:S(2)}, u32[]{:S(2)}) collective-permute-start(f32[2,2,32,128]{3,2,1,0:T(8,128)S(1)} %shard_map.66), channel_id=1, source_target_pairs={{0,17},{1,16},{16,1},{17,0},{2,19},{3,18},{18,3},{19,2},{4,21},{5,... | collective-permute-start | bytes 196616 | tf_op jit(solution)/shard_map/ppermute | solution.py:313
  41.6 6.6 %collective-permute-start.5 = (f32[2,4,32,128]{3,2,1,0:T(8,128)S(1)}, f32[2,4,32,128]{3,2,1,0:T(8,128)S(1)}, u32[]{:S(2)}, u32[]{:S(2)}) collective-permute-start(f32[2,4,32,128]{3,2,1,0:T(8,128)S(1)} %shard_map.68.refs_0_), channel_id=1, source_target_pairs={{0,1},{1,0},{2,3},{3,2},{4,5},{5,4},{6,7},{7,6},{8,9},{9,8},{10,11... | collective-permute-start | bytes 393224 | tf_op jit(solution)/shard_map/ppermute | solution.py:321
  43.8 3.5 %collective-permute-start.7 = (f32[2,1,32,128]{3,2,1,0:T(8,128)S(1)}, f32[2,1,32,128]{3,2,1,0:T(8,128)S(1)}, u32[]{:S(2)}, u32[]{:S(2)}) collective-permute-start(f32[2,1,32,128]{3,2,1,0:T(8,128)S(1)} %shard_map.69), channel_id=1, source_target_pairs={{0,17},{1,16},{16,1},{17,0},{2,19},{3,18},{18,3},{19,2},{4,21},{5,... | collective-permute-start | bytes 98312 | tf_op jit(solution)/shard_map/ppermute | solution.py:316
  43.8 4.4 %collective-permute-start.6 = (f32[2,1,32,128]{3,2,1,0:T(8,128)S(1)}, f32[2,1,32,128]{3,2,1,0:T(8,128)S(1)}, u32[]{:S(2)}, u32[]{:S(2)}) collective-permute-start(f32[2,1,32,128]{3,2,1,0:T(8,128)S(1)} %shard_map.69), channel_id=1, source_target_pairs={{0,16},{1,17},{16,0},{17,1},{2,18},{3,19},{18,2},{19,3},{4,20},{5,... | collective-permute-start | bytes 98312 | tf_op jit(solution)/shard_map/ppermute | solution.py:316
  48.2 3.7 %collective-permute-start.8 = (f32[6,128]{1,0:T(8,128)S(1)}, f32[6,128]{1,0:T(8,128)S(1)}, u32[]{:S(2)}, u32[]{:S(2)}) collective-permute-start(f32[6,128]{1,0:T(8,128)S(1)} %get-tuple-element.24), channel_id=1, source_target_pairs={{0,2},{2,0},{1,3},{3,1},{4,6},{6,4},{5,7},{7,5},{8,10},{10,8},{9,1... | collective-permute-start | bytes 9224 | tf_op jit(solution)/shard_map/ppermute | solution.py:326
